TPU v7x, 32 devices: a whole 2x2x4 slice. The times are simulated.
32 devices in a mesh: dp: 4 (over x, core), head: 4 (over z), expert: 2 (over y).
Axes of the slice: x: 2, y: 2, z: 4, core: 2. Of those that a mesh axis runs over, the one named last changes fastest.
Arguments:
- tokens: bfloat16 [4, 64, 4096], P('dp', ('head', 'expert')), may hold values from -6 to 6
- cotangent: bfloat16 [4, 64, 4096], P('dp', ('head', 'expert')), may hold values from -1.5 to 1.5
- queries: bfloat16 [4, 64, 32, 128], P('dp', 'expert', 'head'), may hold values from -32 to 32
- key_vectors: bfloat16 [4, 64, 32, 128], P('dp', 'expert', 'head'), may hold values from -32 to 32
- value_routes: int32 [4, 32, 64, 1], P('dp', 'head'), may hold values from 0 to 3; in each aligned block of 8 rows (0 to 7, 8 to 15, ..., all dimensions but the last counted through in order) at most 3 rows name the same one
- output_routes: int32 [4, 32, 64, 1], P('dp', 'head'), may hold values from 0 to 3; in each aligned block of 8 rows (0 to 7, 8 to 15, ..., all dimensions but the last counted through in order) at most 3 rows name the same one
- value_experts: bfloat16 [128, 4096, 128], P(('head', 'expert')), may hold values from -0.09375 to 0.09375
- output_experts: bfloat16 [128, 4096, 128], P(('head', 'expert')), may hold values from -0.09375 to 0.09375
Outputs:
- token_grads: bfloat16 [4, 64, 4096], P('dp', ('head', 'expert'))
- query_grads: bfloat16 [4, 64, 32, 128], P('dp', 'expert', 'head')
- key_grads: bfloat16 [4, 64, 32, 128], P('dp', 'expert', 'head')
- value_grads: bfloat16 [128, 4096, 128], P(('head', 'expert'), 'dp')
- output_grads: bfloat16 [128, 4096, 128], P(('head', 'expert'), 'dp')
Inputs may be any that keep to these rules, and one draw needn't show every extreme that they name: value_routes[b, h, t, 0] is the value expert of head h for token t. In each aligned block of 8 tokens of one sequence and head, no expert is chosen more than 3 times, and in every draw some block has exactly 3 for one expert. output_routes[b, h, t, 0] is the output expert of head h for token t. In each aligned block of 8 tokens of one sequence and head, no expert is chosen more than 3 times, and in every draw some block has exactly 3 for one expert.
All inputs are finite; a program needn't handle non-finite values.
Results may differ from a plain program's by a relative error of at most 0.028.
Values may be sent and summed in bfloat16 or wider, within the bound.
A program may use at most 128 MiB of HBM per device.

v0:
```python
import functools

import jax
import jax.numpy as jnp
from jax import lax
from jax.experimental import pallas as pl
from jax.experimental.pallas import tpu as pltpu
from jax.sharding import PartitionSpec as P

E = 4
CAP = 3


def slot_rank(routes):
    onehot = (routes[..., None] == jnp.arange(E, dtype=jnp.int32)).astype(jnp.int32)
    before = jnp.cumsum(onehot, axis=-2) - onehot
    return jnp.sum(before * onehot, axis=-1)


def slot_table(routes):
    rank_of = slot_rank(routes)
    expert_hit = routes[..., None, None, :] == jnp.arange(E, dtype=jnp.int32)[:, None, None]
    place_hit = rank_of[..., None, None, :] == jnp.arange(CAP, dtype=jnp.int32)[:, None]
    return jnp.logical_and(expert_hit, place_hit).astype(jnp.bfloat16)


def local(
    tokens,
    cotangent,
    queries,
    key_vectors,
    value_routes,
    output_routes,
    value_experts,
    output_experts,
):
    head_count = lax.axis_size("head")
    expert_count = lax.axis_size("expert")
    sources = head_count * expert_count
    expert_index = lax.axis_index("expert")
    tok_rows = tokens.shape[1]
    model_width = tokens.shape[2]
    query_rows = queries.shape[1]
    groups = queries.shape[2]
    head_dim = queries.shape[3]
    seq_len = value_routes.shape[2]
    pairs_dev = value_experts.shape[0]
    slot_count = sources * CAP
    score_scale = head_dim ** (-0.5)
    value_local = value_routes[0, :, :, 0]
    output_local = output_routes[0, :, :, 0]

    def own_block(route_part):
        shaped = route_part.reshape(groups, head_count, expert_count, tok_rows)
        return lax.dynamic_index_in_dim(shaped, expert_index, 2, keepdims=False)

    own_pair = jnp.stack([own_block(value_local), own_block(output_local)])
    own_routes = lax.all_to_all(own_pair, "head", split_axis=2, concat_axis=1, tiled=True).reshape(
        2, groups * head_count, tok_rows
    )
    value_table = slot_table(own_routes[0]).reshape(
        head_count, expert_count, pairs_dev, CAP, tok_rows
    )

    def pair_rows(route_part, gathered):
        slot_map = slot_table(route_part.reshape(groups, sources, tok_rows))
        slot_map = jnp.moveaxis(slot_map, 2, 1).reshape(groups * E, sources, CAP, tok_rows)
        slot_map = lax.dynamic_slice_in_dim(slot_map, expert_index * pairs_dev, pairs_dev, 0)
        picked = jnp.einsum(
            "psmt,stw->psmw",
            slot_map,
            gathered.reshape(sources, tok_rows, model_width),
            preferred_element_type=jnp.float32,
        )
        return picked.astype(jnp.bfloat16).reshape(pairs_dev, slot_count, model_width)

    whole_tokens, whole_cotangent = (
        lax.all_gather(tokens[0], ("head", "expert"), axis=0, tiled=True),
        lax.all_gather(cotangent[0], ("head", "expert"), axis=0, tiled=True),
    )
    token_slots = pair_rows(value_local, whole_tokens)
    cotangent_slots = pair_rows(output_local, whole_cotangent)
    value_slots = jnp.einsum(
        "prw,pwk->prk", token_slots, value_experts, preferred_element_type=jnp.float32
    ).astype(jnp.bfloat16)
    upstream_slots = jnp.einsum(
        "prw,pwk->prk", cotangent_slots, output_experts, preferred_element_type=jnp.float32
    ).astype(jnp.bfloat16)
    query_start = expert_index * query_rows
    group_values, group_upstream, all_keys = (
        lax.all_gather(value_slots, "expert", axis=0, tiled=True),
        lax.all_gather(upstream_slots, "expert", axis=0, tiled=True),
        lax.all_gather(key_vectors[0], "expert", axis=0, tiled=True),
    )
    token_source = jnp.arange(seq_len, dtype=jnp.int32) // tok_rows
    head_base = jnp.arange(groups, dtype=jnp.int32)[:, None] * E
    value_rank = slot_rank(value_local.reshape(groups, sources, tok_rows)).reshape(groups, seq_len)
    value_index = (head_base + value_local) * slot_count + token_source * CAP + value_rank
    value_rows = group_values.reshape(-1, head_dim)[value_index]
    output_rank = slot_rank(output_local.reshape(groups, sources, tok_rows)).reshape(
        groups, seq_len
    )
    block_routes = lax.dynamic_slice_in_dim(output_local, query_start, query_rows, 1)
    block_rank = lax.dynamic_slice_in_dim(output_rank, query_start, query_rows, 1)
    block_source = lax.dynamic_slice_in_dim(token_source, query_start, query_rows, 0)
    upstream_index = (head_base + block_routes) * slot_count + block_source * CAP + block_rank
    upstream_rows = group_upstream.reshape(-1, head_dim)[upstream_index]
    query_own = queries[0]
    scores = (
        jnp.einsum("ihc,jhc->hij", query_own, all_keys, preferred_element_type=jnp.float32)
        * score_scale
    )
    query_pos = query_start + jnp.arange(query_rows, dtype=jnp.int32)
    causal = jnp.arange(seq_len, dtype=jnp.int32)[None, :] <= query_pos[:, None]
    row_top = jnp.max(jnp.where(causal, scores, -jnp.inf), axis=-1, keepdims=True)
    weights = jnp.where(causal, jnp.exp(scores - row_top), 0.0)
    probs_full = weights / jnp.sum(weights, axis=-1, keepdims=True)
    prob_half = probs_full.astype(jnp.bfloat16)
    outputs = jnp.einsum(
        "hij,hjc->hic", prob_half, value_rows, preferred_element_type=jnp.float32
    ).astype(jnp.bfloat16)
    row_delta = jnp.sum(outputs.astype(jnp.float32) * upstream_rows.astype(jnp.float32), axis=-1)
    prob_grads = jnp.einsum(
        "hic,hjc->hij", upstream_rows, value_rows, preferred_element_type=jnp.float32
    )
    score_grads = (probs_full * (prob_grads - row_delta[:, :, None])).astype(jnp.bfloat16)
    query_grads = (
        jnp.einsum("hij,jhc->ihc", score_grads, all_keys, preferred_element_type=jnp.float32)
        * score_scale
    ).astype(jnp.bfloat16)
    key_part = (
        jnp.einsum("hij,ihc->jhc", score_grads, query_own, preferred_element_type=jnp.float32)
        * score_scale
    )
    value_part = jnp.einsum(
        "hij,hic->jhc", prob_half, upstream_rows, preferred_element_type=jnp.float32
    )
    key_sum, value_sum = (
        lax.psum_scatter(key_part, "expert", scatter_dimension=0, tiled=True),
        lax.psum_scatter(value_part, "expert", scatter_dimension=0, tiled=True),
    )
    value_half = value_sum.astype(jnp.bfloat16)
    block_value_routes = lax.dynamic_slice_in_dim(value_local, query_start, query_rows, 1).reshape(
        groups, head_count, tok_rows
    )
    value_place = slot_table(block_value_routes)
    output_place = slot_table(block_routes.reshape(groups, head_count, tok_rows))
    value_send = jnp.einsum(
        "hsemt,sthc->hesmc",
        value_place,
        value_half.reshape(head_count, tok_rows, groups, head_dim),
        preferred_element_type=jnp.float32,
    )
    value_send = value_send.astype(jnp.bfloat16).reshape(groups * E, head_count * CAP, head_dim)
    output_send = jnp.einsum(
        "hsemt,hstc->hesmc",
        output_place,
        outputs.reshape(groups, head_count, tok_rows, head_dim),
        preferred_element_type=jnp.float32,
    )
    output_send = output_send.astype(jnp.bfloat16).reshape(groups * E, head_count * CAP, head_dim)
    output_slots, grad_slots = (
        lax.all_to_all(output_send, "expert", split_axis=0, concat_axis=1, tiled=True),
        lax.all_to_all(value_send, "expert", split_axis=0, concat_axis=1, tiled=True),
    )
    value_term = jnp.einsum(
        "prw,prk->pwk", token_slots, grad_slots, preferred_element_type=jnp.float32
    )
    output_term = jnp.einsum(
        "prw,prk->pwk", cotangent_slots, output_slots, preferred_element_type=jnp.float32
    )
    value_grads, output_grads = (
        lax.psum_scatter(
            value_term.astype(jnp.bfloat16), "dp", scatter_dimension=1, tiled=True
        ).astype(jnp.float32),
        lax.psum_scatter(
            output_term.astype(jnp.bfloat16), "dp", scatter_dimension=1, tiled=True
        ).astype(jnp.float32),
    )
    token_terms = jnp.einsum(
        "prk,pwk->prw", grad_slots, value_experts, preferred_element_type=jnp.float32
    ).astype(jnp.bfloat16)
    returned = lax.all_to_all(
        token_terms.reshape(pairs_dev, sources, CAP, model_width),
        ("head", "expert"),
        split_axis=1,
        concat_axis=0,
        tiled=True,
    )
    returned = returned.reshape(head_count, expert_count, pairs_dev, CAP, model_width)
    token_grads = jnp.einsum(
        "gjpmt,gjpmw->tw", value_table, returned, preferred_element_type=jnp.float32
    )
    return (
        token_grads.astype(jnp.bfloat16)[None],
        query_grads[None],
        key_sum.astype(jnp.bfloat16)[None],
        value_grads.astype(jnp.bfloat16),
        output_grads.astype(jnp.bfloat16),
    )


def fused_kernel(
    sizes,
    tok,
    cot,
    q_in,
    k_in,
    routes_in,
    value_hbm,
    output_hbm,
    tok_out,
    qg_out,
    kg_out,
    flat_out,
    masked_out,
    rows,
    flat,
    flat_t,
    by_heads,
    routes,
    weight,
    heads_in,
    part,
    part_in,
    factor,
    masked,
    score_keep,
    prob_keep,
    upstream_keep,
    back,
    back_in,
    term,
    term_in,
    sem_weight,
    sem_own,
    sem_rows,
    sem_routes,
    sem_line,
    sem_side,
    sem_heads,
    sem_part,
    sem_factor,
    sem_back,
    sem_term,
    sem_grads,
):
    dn, gn, jn, own_heads, query_rows, tok_rows, width, head_dim = sizes
    sources = gn * jn
    seq_len = sources * tok_rows
    scale = head_dim ** (-0.5)
    d, g, j = lax.axis_index("dp"), lax.axis_index("head"), lax.axis_index("expert")
    block = g * jn + j
    f32, bf16 = jnp.float32, jnp.bfloat16

    def at(dd, gg, jj):
        return {"dp": lax.rem(d + dd, dn), "head": lax.rem(g + gg, gn), "expert": lax.rem(j + jj, jn)}

    others = [
        (dd, gg, jj)
        for dd in range(dn)
        for gg in range(gn)
        for jj in range(jn)
        if (dd, gg, jj) != (0, 0, 0)
    ]
    sent = []

    def send(src, dst, sems, slot, where):
        copy = pltpu.make_async_remote_copy(
            src_ref=src,
            dst_ref=dst,
            send_sem=sems.at[(0,) + slot],
            recv_sem=sems.at[(1,) + slot],
            device_id=at(*where),
            device_id_type=pl.DeviceIdType.MESH,
        )
        copy.start()
        sent.append(copy)
        return copy

    def columns(index):
        return pl.ds(pl.multiple_of(index * width, 128), width)

    weights_on_way = [
        pltpu.make_async_copy(hbm.at[:, columns(d), :], weight.at[i], sem_weight.at[i])
        for i, hbm in enumerate((value_hbm, output_hbm))
    ]
    for copy in weights_on_way:
        copy.start()
    own = [
        pltpu.make_async_copy(tok.at[:, columns(d)], rows.at[block, 0, d], sem_own.at[0]),
        pltpu.make_async_copy(cot.at[:, columns(d)], rows.at[block, 1, d], sem_own.at[1]),
        pltpu.make_async_copy(routes_in, routes.at[d], sem_own.at[2]),
    ]
    for copy in own:
        copy.start()

    barrier = pltpu.get_barrier_semaphore()
    for where in others:
        pl.semaphore_signal(
            barrier, inc=1, device_id=at(*where), device_id_type=pl.DeviceIdType.MESH
        )
    pl.semaphore_wait(barrier, len(others))

    first, late, line, side = [[], []], [], [[], []], [[], []]
    for i in (1, 0):
        for dd in range(1, dn):
            target = columns(lax.rem(d + dd, dn))
            source = (tok, cot)[i]
            first[i].append(
                send(source.at[:, target], rows.at[block, i, d], sem_rows, (dd, i), (dd, 0, 0))
            )
        if i == 1:
            late = [
                send(routes_in, routes.at[d], sem_routes, (dd,), (dd, 0, 0))
                for dd in range(1, dn)
            ]
    for copy in own:
        copy.wait()
    for i in (1, 0):
        for copy in first[i]:
            copy.wait_recv()
        here = rows.at[block, i]
        for gg in range(1, gn):
            line[i].append(send(here, here, sem_line, (gg, i), (0, gg, 0)))
        for jj in range(1, jn):
            side[i].append(send(here, here, sem_side, (0, jj, i), (0, 0, jj)))
    for i, source in enumerate((q_in, k_in)):
        turned = jnp.transpose(source[...].astype(f32), (1, 0, 2)).astype(bf16)
        for jj in range(jn):
            by_heads[i, jj] = turned[jj * own_heads : (jj + 1) * own_heads]
        heads_in[i, j] = by_heads[i, j]
    swapped = []
    for jj in range(1, jn):
        peer = lax.rem(j + jj, jn)
        for i in range(2):
            swapped.append(
                send(by_heads.at[i, peer], heads_in.at[i, j], sem_heads, (i, jj), (0, 0, jj))
            )

    def forward(i):
        for gg in range(1, gn):
            line[i][gg - 1].wait_recv()
            came = rows.at[lax.rem(g + gn - gg, gn) * jn + j, i]
            for jj in range(1, jn):
                side[i].append(send(came, came, sem_side, (gg, jj, i), (0, 0, jj)))

    def flatten(i):
        for copy in side[i]:
            copy.wait_recv()
        for b in range(dn):
            piece = jnp.concatenate([rows[s, i, b].astype(f32) for s in range(sources)], axis=0)
            flat[i, b * seq_len : (b + 1) * seq_len, :] = piece.astype(bf16)

    def column(i, h, b):
        c = i * own_heads + h
        return jnp.broadcast_to(routes[b, :, c : c + 1], (seq_len, head_dim))

    def project(i):
        weights_on_way[i].wait()
        for h in range(own_heads):
            picked = [jnp.zeros((seq_len, head_dim), f32) for _ in range(dn)]
            for e in range(0, E, 2):
                p = h * E + e
                both = jnp.concatenate([weight[i, p], weight[i, p + 1]], axis=1)
                every = jnp.dot(flat[i], both, preferred_element_type=f32)
                for b in range(dn):
                    own_rows = every[b * seq_len : (b + 1) * seq_len]
                    route = column(i, h, b)
                    picked[b] = jnp.where(route == e, own_rows[:, :head_dim], picked[b])
                    picked[b] = jnp.where(route == e + 1, own_rows[:, head_dim:], picked[b])
            for b in range(dn):
                part[b, i, h] = picked[b].astype(bf16)
        return [
            send(
                part.at[lax.rem(d + dd, dn), i], part_in.at[dd, i], sem_part, (dd, i), (dd, 0, 0)
            )
            for dd in range(1, dn)
        ]

    forward(1)
    flatten(1)
    for copy in late:
        copy.wait_recv()
    upstream_on_way = project(1)
    forward(0)

    query_pos = lax.broadcasted_iota(jnp.int32, (seq_len, seq_len), 0)
    key_pos = lax.broadcasted_iota(jnp.int32, (seq_len, seq_len), 1)
    causal = key_pos <= query_pos

    def joined(i, h):
        return jnp.concatenate([heads_in[i, jj, h] for jj in range(jn)], axis=0)

    def total(i, h):
        whole = part[d, i, h].astype(f32)
        for dd in range(1, dn):
            whole = whole + part_in[dd, i, h].astype(f32)
        return whole.astype(bf16)

    def across(a, b):
        return lax.dot_general(a, b, (((1,), (1,)), ((), ())), preferred_element_type=f32)

    def over_rows(a, b):
        return lax.dot_general(a, b, (((0,), (0,)), ((), ())), preferred_element_type=f32)

    def mask(i):
        for h in range(own_heads):
            for b in range(dn):
                source = factor[b, i, h].astype(f32)
                route = column(i, h, b)
                for e in range(E):
                    p = h * E + e
                    masked[
                        i,
                        p // 2,
                        b * seq_len : (b + 1) * seq_len,
                        (p % 2) * head_dim : (p % 2 + 1) * head_dim,
                    ] = jnp.where(route == e, source, 0.0).astype(bf16)

    def spread(i):
        return [
            send(factor.at[d, i], factor.at[d, i], sem_factor, (dd, i), (dd, 0, 0))
            for dd in range(1, dn)
        ]

    for copy in swapped:
        copy.wait_recv()
    for h in range(own_heads):
        query, key = joined(0, h), joined(1, h)
        scores = across(query, key) * scale
        top = jnp.max(jnp.where(causal, scores, -jnp.inf), axis=-1, keepdims=True)
        soft = jnp.where(causal, jnp.exp(scores - top), 0.0)
        prob_keep[h] = soft / jnp.sum(soft, axis=-1, keepdims=True)
    for copy in upstream_on_way:
        copy.wait_recv()
    for h in range(own_heads):
        upstream_keep[h] = total(1, h)
        factor[d, 0, h] = over_rows(prob_keep[h].astype(bf16), upstream_keep[h]).astype(bf16)
    value_spread = spread(0)
    flatten(0)
    values_on_way = project(0)
    for copy in value_spread:
        copy.wait_recv()
    mask(0)
    couples = own_heads * E // 2
    step = min(width, 256)
    for n in range(0, width, step):
        added = jnp.zeros((dn * seq_len, step), f32)
        for c in range(couples):
            both = jnp.concatenate(
                [weight[0, 2 * c, n : n + step, :], weight[0, 2 * c + 1, n : n + step, :]], axis=1
            )
            added = added + across(masked[0, c], both)
        for r in range(dn * sources):
            term[r, :, n : n + step] = added[r * tok_rows : (r + 1) * tok_rows].astype(bf16)
    terms = []
    for slot, (dd, gg, jj) in enumerate(others):
        target = (
            lax.rem(d + dd, dn) * sources + lax.rem(g + gg, gn) * jn + lax.rem(j + jj, jn)
        )
        terms.append(
            send(term.at[target], term_in.at[d * sources + block], sem_term, (slot,), (dd, gg, jj))
        )
    term_in[d * sources + block] = term[d * sources + block]

    for copy in values_on_way:
        copy.wait_recv()
    for h in range(own_heads):
        value, upstream, probs = total(0, h), upstream_keep[h], prob_keep[h]
        output = jnp.dot(probs.astype(bf16), value, preferred_element_type=f32).astype(bf16)
        factor[d, 1, h] = output
        delta = jnp.sum(output.astype(f32) * upstream.astype(f32), axis=-1, keepdims=True)
        score_keep[h] = (probs * (across(upstream, value) - delta)).astype(bf16)
    output_spread = spread(1)
    for h in range(own_heads):
        query, key, score = joined(0, h), joined(1, h), score_keep[h]
        query_grad = (jnp.dot(score, key, preferred_element_type=f32) * scale).astype(bf16)
        key_grad = (over_rows(score, query) * scale).astype(bf16)
        for jj in range(jn):
            back[jj, 0, h] = query_grad[jj * query_rows : (jj + 1) * query_rows]
            back[jj, 1, h] = key_grad[jj * query_rows : (jj + 1) * query_rows]
    returned = [
        send(back.at[lax.rem(j + jj, jn)], back_in.at[j], sem_back, (jj,), (0, 0, jj))
        for jj in range(1, jn)
    ]
    for i in range(2):
        flat_t[i] = flat[i].T
    for copy in output_spread:
        copy.wait_recv()
    mask(1)
    outgoing = [
        pltpu.make_async_copy(flat_t, flat_out, sem_grads.at[0]),
        pltpu.make_async_copy(masked, masked_out, sem_grads.at[1]),
    ]
    for copy in outgoing:
        copy.start()

    back_in[j] = back[j]
    for copy in returned:
        copy.wait_recv()
    for jj in range(jn):
        qg_out[jj] = back_in[jj, 0]
        kg_out[jj] = back_in[jj, 1]
    for copy in terms:
        copy.wait_recv()
    for b in range(dn):
        total_rows = term_in[b * sources].astype(f32)
        for s in range(1, sources):
            total_rows = total_rows + term_in[b * sources + s].astype(f32)
        tok_out[:, b * width : (b + 1) * width] = total_rows.astype(bf16)
    for copy in outgoing:
        copy.wait()
    for copy in sent:
        copy.wait_send()


def finish_kernel(flat_t, masked, tok_in, qg_in, kg_in, tok_out, qg_out, kg_out, vg_out, og_out):
    @pl.when(pl.program_id(0) == 0)
    def _():
        tok_out[...] = tok_in[...]
        for source, out in ((qg_in, qg_out), (kg_in, kg_out)):
            out[...] = jnp.transpose(source[...].astype(jnp.float32), (1, 0, 2)).astype(out.dtype)

    half = masked.shape[-1] // 2
    for i, out in enumerate((vg_out, og_out)):
        for c in range(masked.shape[1]):
            whole = jnp.dot(flat_t[i], masked[i, c], preferred_element_type=jnp.float32)
            out[2 * c] = whole[:, :half].astype(out.dtype)
            out[2 * c + 1] = whole[:, half:].astype(out.dtype)


def fused(
    tokens,
    cotangent,
    queries,
    key_vectors,
    value_routes,
    output_routes,
    value_experts,
    output_experts,
):
    dn, gn, jn = lax.axis_size("dp"), lax.axis_size("head"), lax.axis_size("expert")
    expert_index = lax.axis_index("expert")
    _, tok_rows, model_width = tokens.shape
    width = model_width // dn
    _, query_rows, groups, head_dim = queries.shape
    seq_len = value_routes.shape[2]
    pairs_dev = value_experts.shape[0]
    own_heads = groups // jn
    sources = gn * jn
    bf16 = jnp.bfloat16

    routes = jnp.concatenate(
        [
            lax.dynamic_slice_in_dim(route[0, :, :, 0], expert_index * own_heads, own_heads, 0)
            for route in (value_routes, output_routes)
        ]
    )
    routes = jnp.pad(routes.T, ((0, 0), (0, 128 - 2 * own_heads)))

    vmem = pl.BlockSpec(memory_space=pltpu.VMEM)
    hbm = pl.BlockSpec(memory_space=pl.ANY)
    dma = pltpu.SemaphoreType.DMA
    head_block = (jn, own_heads, query_rows, head_dim)
    grad_shape = jax.ShapeDtypeStruct((pairs_dev, width, head_dim), bf16)
    couples, all_rows = pairs_dev // 2, dn * seq_len
    tok_grads, query_grads, key_grads, flat_t, masked = pl.pallas_call(
        functools.partial(
            fused_kernel, (dn, gn, jn, own_heads, query_rows, tok_rows, width, head_dim)
        ),
        name="fused",
        out_shape=(
            jax.ShapeDtypeStruct((tok_rows, model_width), bf16),
            jax.ShapeDtypeStruct(head_block, bf16),
            jax.ShapeDtypeStruct(head_block, bf16),
            jax.ShapeDtypeStruct((2, width, all_rows), bf16),
            jax.ShapeDtypeStruct((2, couples, all_rows, 2 * head_dim), bf16),
        ),
        in_specs=[vmem] * 5 + [hbm] * 2,
        out_specs=(vmem, vmem, vmem, hbm, hbm),
        scratch_shapes=[
            pltpu.VMEM((sources, 2, dn, tok_rows, width), bf16),
            pltpu.VMEM((2, dn * seq_len, width), bf16),
            pltpu.VMEM((2, width, dn * seq_len), bf16),
            pltpu.VMEM((2, jn, own_heads, query_rows, head_dim), bf16),
            pltpu.VMEM((dn, seq_len, 128), jnp.int32),
            pltpu.VMEM((2, pairs_dev, width, head_dim), bf16),
            pltpu.VMEM((2, jn, own_heads, query_rows, head_dim), bf16),
            pltpu.VMEM((dn, 2, own_heads, seq_len, head_dim), bf16),
            pltpu.VMEM((dn, 2, own_heads, seq_len, head_dim), bf16),
            pltpu.VMEM((dn, 2, own_heads, seq_len, head_dim), bf16),
            pltpu.VMEM((2, pairs_dev // 2, dn * seq_len, 2 * head_dim), bf16),
            pltpu.VMEM((own_heads, seq_len, seq_len), bf16),
            pltpu.VMEM((own_heads, seq_len, seq_len), jnp.float32),
            pltpu.VMEM((own_heads, seq_len, head_dim), bf16),
            pltpu.VMEM((jn, 2, own_heads, query_rows, head_dim), bf16),
            pltpu.VMEM((jn, 2, own_heads, query_rows, head_dim), bf16),
            pltpu.VMEM((dn * sources, tok_rows, width), bf16),
            pltpu.VMEM((dn * sources, tok_rows, width), bf16),
            dma((2,)),
            dma((3,)),
            dma((2, dn, 2)),
            dma((2, dn)),
            dma((2, gn, 2)),
            dma((2, gn, jn, 2)),
            dma((2, 2, jn)),
            dma((2, dn, 2)),
            dma((2, dn, 2)),
            dma((2, jn)),
            dma((2, dn * sources)),
            dma((2,)),
        ],
        compiler_params=pltpu.CompilerParams(
            collective_id=0, has_side_effects=True, vmem_limit_bytes=60 * 1024 * 1024
        ),
    )(
        tokens[0],
        cotangent[0],
        queries[0],
        key_vectors[0],
        routes,
        value_experts,
        output_experts,
    )

    def fixed(shape):
        return pl.BlockSpec(shape, lambda c: (0,) * len(shape))

    per = 2 if couples % 2 == 0 else 1
    by_head = (groups, query_rows, head_dim)
    by_row = (query_rows, groups, head_dim)
    grad_block = pl.BlockSpec((2 * per, width, head_dim), lambda c: (c, 0, 0))
    row_shape = jax.ShapeDtypeStruct(by_row, bf16)
    tok_grads, query_grads, key_grads, value_grads, output_grads = pl.pallas_call(
        finish_kernel,
        name="finish",
        grid=(couples // per,),
        out_shape=(
            jax.ShapeDtypeStruct((tok_rows, model_width), bf16),
            row_shape,
            row_shape,
            grad_shape,
            grad_shape,
        ),
        in_specs=[
            fixed((2, width, all_rows)),
            pl.BlockSpec((2, per, all_rows, 2 * head_dim), lambda c: (0, c, 0, 0)),
            fixed((tok_rows, model_width)),
            fixed(by_head),
            fixed(by_head),
        ],
        out_specs=(
            fixed((tok_rows, model_width)),
            fixed(by_row),
            fixed(by_row),
            grad_block,
            grad_block,
        ),
        compiler_params=pltpu.CompilerParams(vmem_limit_bytes=60 * 1024 * 1024),
    )(flat_t, masked, tok_grads, query_grads.reshape(by_head), key_grads.reshape(by_head))
    return tok_grads[None], query_grads[None], key_grads[None], value_grads, output_grads


def chosen(*args):
    groups, pairs_dev = args[2].shape[2], args[6].shape[0]
    dp_count, expert_count = lax.axis_size("dp"), lax.axis_size("expert")
    whole_heads = groups % expert_count == 0 and pairs_dev == groups // expert_count * E
    if whole_heads and args[0].shape[2] % (dp_count * 256) == 0 and args[2].shape[1] <= 64:
        return fused(*args)
    return local(*args)


def solution(mesh):
    return jax.shard_map(
        chosen,
        mesh=mesh,
        in_specs=(
            P("dp", ("head", "expert"), None),
            P("dp", ("head", "expert"), None),
            P("dp", "expert", "head", None),
            P("dp", "expert", "head", None),
            P("dp", "head", None, None),
            P("dp", "head", None, None),
            P(("head", "expert"), None, None),
            P(("head", "expert"), None, None),
        ),
        out_specs=(
            P("dp", ("head", "expert"), None),
            P("dp", "expert", "head", None),
            P("dp", "expert", "head", None),
            P(("head", "expert"), "dp", None),
            P(("head", "expert"), "dp", None),
        ),
        check_vma=False,
    )
```

profile of v0, /device:TPU:25, one launch (start us, length us, event | category | flops | bytes accessed | tf_op | source)
XLA Modules:
  0.0 57.0 jit_solution(7977124402863800083)
XLA Ops:
  0.6 0.7 %constant_dynamic-slice_fusion = (s32[1,4,64,1]{2,3,1,0:T(1,128)S(1)}, s32[1,4,64,1]{2,3,1,0:T(1,128)S(1)}) fusion(s32[1,8,64,1]{2,3,1,0:T(1,128)} %param.13, s32[]{:T(128)S(6)} %select_n.4, s32[1,8,64,1]{2,3,1,0:T(1,128)} %param.12), kind=kLoop, calls=%fused_computation.1 | loop fusion | bytes 4100 | tf_op jit(solution)/shard_map/dynamic_slice | solution.py:556
  1.4 0.1 copy.15
  1.4 0.6 %pad.4.routes_in = s32[64,128]{1,0:T(8,128)} pad(s32[64,8]{1,0:T(8,128)S(1)} %bitcast.12, s32[]{:T(128)} %constant.4.clone.1), padding=0_0x0_120 | pad | bytes 34820 | tf_op jit(solution)/shard_map/jit(_pad)/pad | solution.py:560
  2.1 48.5 %fused.1 = (bf16[8,4096]{1,0:T(8,128)(2,1)}, bf16[2,4,32,128]{3,2,1,0:T(8,128)(2,1)}, bf16[2,4,32,128]{3,2,1,0:T(8,128)(2,1)}, bf16[2,1024,256]{2,1,0:T(8,128)(2,1)}, bf16[2,8,256,256]{3,2,1,0:T(8,128)(2,1)}) custom-call(bf16[8,4096]{1,0:T(8,128)(2,1)} %bitcast.13, bf16[8,4096]{1,0:T(8,128)(2,1)} %bitcast.14, bf16[32,8,128]{2,1,0:T(8,128)(2,1)} %bitcast.15, ...), custom_call_target="tpu_custom_call" | custom-call | tf_op jit(solution)/shard_map/fused/pallas_call | solution.py:568
  50.6 6.4 %finish.1 = (bf16[8,4096]{1,0:T(8,128)(2,1)}, bf16[32,8,128]{2,1,0:T(8,128)(2,1)}, bf16[32,8,128]{2,1,0:T(8,128)(2,1)}, bf16[16,1024,128]{2,1,0:T(8,128)(2,1)}, bf16[16,1024,128]{2,1,0:T(8,128)(2,1)}) custom-call(bf16[2,1024,256]{2,1,0:T(8,128)(2,1)} %get-tuple-element.15.flat_t, bf16[2,8,256,256]{3,2,1,0:T(8,128)(2,1)} %get-tuple-element.16.masked, ...), custom_call_target="tpu_custom_call" | custom-call | tf_op jit(solution)/shard_map/finish/pallas_call | solution.py:635
  (1 shorter events, 0.0 us)
where the time goes:
time: 57.3 us; the launch traced here: 57 us
  Pallas kernels  54.9 us (96%)
  local copies, waits for them, and re-layouts  1.41 us (2%)
  between operations  0.65 us (1%)
    pallas_call x1, Pallas kernels, fused(): pl.pallas_call(functools.partial(fused_kernel, (dn, gn, jn, own_heads, qu...  48.5 us
    pallas_call x1, Pallas kernels, fused(): pl.pallas_call(finish_kernel, name='finish', grid=(couples // per,), out_...  6.41 us

commit v1 on v0

--- a/solution.py
+++ b/solution.py
@@ -12,9 +12,9 @@
 
 
 def slot_rank(routes):
-    onehot = (routes[..., None] == jnp.arange(E, dtype=jnp.int32)).astype(jnp.int32)
-    before = jnp.cumsum(onehot, axis=-2) - onehot
-    return jnp.sum(before * onehot, axis=-1)
+    places = jnp.arange(routes.shape[-1], dtype=jnp.int32)
+    same = routes[..., :, None] == routes[..., None, :]
+    return jnp.sum(jnp.logical_and(same, places[None, :] < places[:, None]).astype(jnp.int32), axis=-1)
 
 
 def slot_table(routes):
@@ -206,19 +206,22 @@
     cot,
     q_in,
     k_in,
-    routes_in,
+    value_routes_in,
+    output_routes_in,
     value_hbm,
     output_hbm,
     tok_out,
     qg_out,
     kg_out,
-    flat_out,
-    masked_out,
+    vg_out,
+    og_out,
     rows,
     flat,
     flat_t,
+    heads_raw,
     by_heads,
     routes,
+    route_columns,
     weight,
     heads_in,
     part,
@@ -243,7 +246,6 @@
     sem_factor,
     sem_back,
     sem_term,
-    sem_grads,
 ):
     dn, gn, jn, own_heads, query_rows, tok_rows, width, head_dim = sizes
     sources = gn * jn
@@ -285,12 +287,21 @@
         pltpu.make_async_copy(hbm.at[:, columns(d), :], weight.at[i], sem_weight.at[i])
         for i, hbm in enumerate((value_hbm, output_hbm))
     ]
-    for copy in weights_on_way:
-        copy.start()
     own = [
         pltpu.make_async_copy(tok.at[:, columns(d)], rows.at[block, 0, d], sem_own.at[0]),
         pltpu.make_async_copy(cot.at[:, columns(d)], rows.at[block, 1, d], sem_own.at[1]),
-        pltpu.make_async_copy(routes_in, routes.at[d], sem_own.at[2]),
+        pltpu.make_async_copy(
+            value_routes_in.at[pl.ds(j * own_heads, own_heads)],
+            routes.at[d, pl.ds(0, own_heads)],
+            sem_own.at[2],
+        ),
+        pltpu.make_async_copy(
+            output_routes_in.at[pl.ds(j * own_heads, own_heads)],
+            routes.at[d, pl.ds(own_heads, own_heads)],
+            sem_own.at[3],
+        ),
+        pltpu.make_async_copy(q_in, heads_raw.at[0], sem_own.at[4]),
+        pltpu.make_async_copy(k_in, heads_raw.at[1], sem_own.at[5]),
     ]
     for copy in own:
         copy.start()
@@ -310,13 +321,13 @@
             first[i].append(
                 send(source.at[:, target], rows.at[block, i, d], sem_rows, (dd, i), (dd, 0, 0))
             )
-        if i == 1:
-            late = [
-                send(routes_in, routes.at[d], sem_routes, (dd,), (dd, 0, 0))
-                for dd in range(1, dn)
-            ]
+    for copy in weights_on_way:
+        copy.start()
     for copy in own:
         copy.wait()
+    late = [
+        send(routes.at[d], routes.at[d], sem_routes, (dd,), (dd, 0, 0)) for dd in range(1, dn)
+    ]
     for i in (1, 0):
         for copy in first[i]:
             copy.wait_recv()
@@ -325,8 +336,8 @@
             line[i].append(send(here, here, sem_line, (gg, i), (0, gg, 0)))
         for jj in range(1, jn):
             side[i].append(send(here, here, sem_side, (0, jj, i), (0, 0, jj)))
-    for i, source in enumerate((q_in, k_in)):
-        turned = jnp.transpose(source[...].astype(f32), (1, 0, 2)).astype(bf16)
+    for i in range(2):
+        turned = jnp.transpose(heads_raw[i].astype(f32), (1, 0, 2)).astype(bf16)
         for jj in range(jn):
             by_heads[i, jj] = turned[jj * own_heads : (jj + 1) * own_heads]
         heads_in[i, j] = by_heads[i, j]
@@ -354,7 +365,14 @@
 
     def column(i, h, b):
         c = i * own_heads + h
-        return jnp.broadcast_to(routes[b, :, c : c + 1], (seq_len, head_dim))
+        return jnp.broadcast_to(route_columns[b, :seq_len, c : c + 1], (seq_len, head_dim))
+
+    def turn_routes(b):
+        lines = jnp.concatenate([routes[b, c] for c in range(2 * own_heads)], axis=0)
+        spare = route_columns.shape[1] - seq_len
+        if spare:
+            lines = jnp.concatenate([lines, jnp.zeros((2 * own_heads, spare), jnp.int32)], axis=1)
+        route_columns[b] = lines.T
 
     def project(i):
         weights_on_way[i].wait()
@@ -382,6 +400,8 @@
     flatten(1)
     for copy in late:
         copy.wait_recv()
+    for b in range(dn):
+        turn_routes(b)
     upstream_on_way = project(1)
     forward(0)
 
@@ -484,17 +504,19 @@
         send(back.at[lax.rem(j + jj, jn)], back_in.at[j], sem_back, (jj,), (0, 0, jj))
         for jj in range(1, jn)
     ]
-    for i in range(2):
+
+    def gradients(i, out):
         flat_t[i] = flat[i].T
+        for c in range(couples):
+            whole = jnp.dot(flat_t[i], masked[i, c], preferred_element_type=f32)
+            out[2 * c] = whole[:, :head_dim].astype(bf16)
+            out[2 * c + 1] = whole[:, head_dim:].astype(bf16)
+
+    gradients(0, vg_out)
     for copy in output_spread:
         copy.wait_recv()
     mask(1)
-    outgoing = [
-        pltpu.make_async_copy(flat_t, flat_out, sem_grads.at[0]),
-        pltpu.make_async_copy(masked, masked_out, sem_grads.at[1]),
-    ]
-    for copy in outgoing:
-        copy.start()
+    gradients(1, og_out)
 
     back_in[j] = back[j]
     for copy in returned:
@@ -509,25 +531,29 @@
         for s in range(1, sources):
             total_rows = total_rows + term_in[b * sources + s].astype(f32)
         tok_out[:, b * width : (b + 1) * width] = total_rows.astype(bf16)
-    for copy in outgoing:
-        copy.wait()
     for copy in sent:
         copy.wait_send()
 
 
-def finish_kernel(flat_t, masked, tok_in, qg_in, kg_in, tok_out, qg_out, kg_out, vg_out, og_out):
-    @pl.when(pl.program_id(0) == 0)
-    def _():
-        tok_out[...] = tok_in[...]
-        for source, out in ((qg_in, qg_out), (kg_in, kg_out)):
-            out[...] = jnp.transpose(source[...].astype(jnp.float32), (1, 0, 2)).astype(out.dtype)
-
-    half = masked.shape[-1] // 2
-    for i, out in enumerate((vg_out, og_out)):
-        for c in range(masked.shape[1]):
-            whole = jnp.dot(flat_t[i], masked[i, c], preferred_element_type=jnp.float32)
-            out[2 * c] = whole[:, :half].astype(out.dtype)
-            out[2 * c + 1] = whole[:, half:].astype(out.dtype)
+def finish_kernel(
+    tok_in, qg_in, kg_in, vg_in, og_in, tok_out, qg_out, kg_out, vg_out, og_out, turned, sems
+):
+    pieces = sems.shape[1]
+    size = vg_in.shape[0] // (pieces - 1)
+    copies = [pltpu.make_async_copy(tok_in, tok_out, sems.at[0, pieces - 1])]
+    for i, (source, out) in enumerate(((vg_in, vg_out), (og_in, og_out))):
+        for n in range(pieces - 1):
+            part = pl.ds(n * size, size)
+            copies.append(pltpu.make_async_copy(source.at[part], out.at[part], sems.at[i, n]))
+    for copy in copies:
+        copy.start()
+    late = []
+    for i, (source, out) in enumerate(((qg_in, qg_out), (kg_in, kg_out))):
+        turned[i] = jnp.transpose(source[...].astype(jnp.float32), (1, 0, 2)).astype(out.dtype)
+        late.append(pltpu.make_async_copy(turned.at[i], out, sems.at[2, i]))
+        late[i].start()
+    for copy in copies + late:
+        copy.wait()
 
 
 def fused(
@@ -541,7 +567,6 @@
     output_experts,
 ):
     dn, gn, jn = lax.axis_size("dp"), lax.axis_size("head"), lax.axis_size("expert")
-    expert_index = lax.axis_index("expert")
     _, tok_rows, model_width = tokens.shape
     width = model_width // dn
     _, query_rows, groups, head_dim = queries.shape
@@ -551,40 +576,36 @@
     sources = gn * jn
     bf16 = jnp.bfloat16
 
-    routes = jnp.concatenate(
-        [
-            lax.dynamic_slice_in_dim(route[0, :, :, 0], expert_index * own_heads, own_heads, 0)
-            for route in (value_routes, output_routes)
-        ]
-    )
-    routes = jnp.pad(routes.T, ((0, 0), (0, 128 - 2 * own_heads)))
+    value_lines = value_routes.reshape(groups, 1, seq_len)
+    output_lines = output_routes.reshape(groups, 1, seq_len)
 
     vmem = pl.BlockSpec(memory_space=pltpu.VMEM)
     hbm = pl.BlockSpec(memory_space=pl.ANY)
     dma = pltpu.SemaphoreType.DMA
     head_block = (jn, own_heads, query_rows, head_dim)
     grad_shape = jax.ShapeDtypeStruct((pairs_dev, width, head_dim), bf16)
-    couples, all_rows = pairs_dev // 2, dn * seq_len
-    tok_grads, query_grads, key_grads, flat_t, masked = pl.pallas_call(
+    tok_grads, query_grads, key_grads, value_grads, output_grads = pl.pallas_call(
         functools.partial(
             fused_kernel, (dn, gn, jn, own_heads, query_rows, tok_rows, width, head_dim)
         ),
         name="fused",
         out_shape=(
-            jax.ShapeDtypeStruct((tok_rows, model_width), bf16),
-            jax.ShapeDtypeStruct(head_block, bf16),
-            jax.ShapeDtypeStruct(head_block, bf16),
-            jax.ShapeDtypeStruct((2, width, all_rows), bf16),
-            jax.ShapeDtypeStruct((2, couples, all_rows, 2 * head_dim), bf16),
-        ),
-        in_specs=[vmem] * 5 + [hbm] * 2,
-        out_specs=(vmem, vmem, vmem, hbm, hbm),
+            pltpu.VMEM((tok_rows, model_width), bf16),
+            pltpu.VMEM(head_block, bf16),
+            pltpu.VMEM(head_block, bf16),
+            pltpu.VMEM(grad_shape.shape, bf16),
+            pltpu.VMEM(grad_shape.shape, bf16),
+        ),
+        in_specs=[hbm] * 8,
+        out_specs=(vmem,) * 5,
         scratch_shapes=[
             pltpu.VMEM((sources, 2, dn, tok_rows, width), bf16),
             pltpu.VMEM((2, dn * seq_len, width), bf16),
             pltpu.VMEM((2, width, dn * seq_len), bf16),
+            pltpu.VMEM((2, query_rows, groups, head_dim), bf16),
             pltpu.VMEM((2, jn, own_heads, query_rows, head_dim), bf16),
-            pltpu.VMEM((dn, seq_len, 128), jnp.int32),
+            pltpu.VMEM((dn, 2 * own_heads, 1, seq_len), jnp.int32),
+            pltpu.VMEM((dn, -(-seq_len // 128) * 128, 2 * own_heads), jnp.int32),
             pltpu.VMEM((2, pairs_dev, width, head_dim), bf16),
             pltpu.VMEM((2, jn, own_heads, query_rows, head_dim), bf16),
             pltpu.VMEM((dn, 2, own_heads, seq_len, head_dim), bf16),
@@ -599,7 +620,7 @@
             pltpu.VMEM((dn * sources, tok_rows, width), bf16),
             pltpu.VMEM((dn * sources, tok_rows, width), bf16),
             dma((2,)),
-            dma((3,)),
+            dma((6,)),
             dma((2, dn, 2)),
             dma((2, dn)),
             dma((2, gn, 2)),
@@ -609,33 +630,31 @@
             dma((2, dn, 2)),
             dma((2, jn)),
             dma((2, dn * sources)),
-            dma((2,)),
         ],
         compiler_params=pltpu.CompilerParams(
-            collective_id=0, has_side_effects=True, vmem_limit_bytes=60 * 1024 * 1024
+            collective_id=0, has_side_effects=True, vmem_limit_bytes=40 * 1024 * 1024
         ),
     )(
-        tokens[0],
-        cotangent[0],
-        queries[0],
-        key_vectors[0],
-        routes,
+        *(
+            pltpu.with_memory_space_constraint(x, pltpu.HBM)
+            for x in (
+                tokens[0],
+                cotangent[0],
+                queries[0],
+                key_vectors[0],
+                value_lines,
+                output_lines,
+            )
+        ),
         value_experts,
         output_experts,
     )
 
-    def fixed(shape):
-        return pl.BlockSpec(shape, lambda c: (0,) * len(shape))
-
-    per = 2 if couples % 2 == 0 else 1
     by_head = (groups, query_rows, head_dim)
-    by_row = (query_rows, groups, head_dim)
-    grad_block = pl.BlockSpec((2 * per, width, head_dim), lambda c: (c, 0, 0))
-    row_shape = jax.ShapeDtypeStruct(by_row, bf16)
+    row_shape = jax.ShapeDtypeStruct((query_rows, groups, head_dim), bf16)
     tok_grads, query_grads, key_grads, value_grads, output_grads = pl.pallas_call(
         finish_kernel,
         name="finish",
-        grid=(couples // per,),
         out_shape=(
             jax.ShapeDtypeStruct((tok_rows, model_width), bf16),
             row_shape,
@@ -643,22 +662,20 @@
             grad_shape,
             grad_shape,
         ),
-        in_specs=[
-            fixed((2, width, all_rows)),
-            pl.BlockSpec((2, per, all_rows, 2 * head_dim), lambda c: (0, c, 0, 0)),
-            fixed((tok_rows, model_width)),
-            fixed(by_head),
-            fixed(by_head),
+        in_specs=[vmem] * 5,
+        out_specs=(hbm,) * 5,
+        scratch_shapes=[
+            pltpu.VMEM((2, query_rows, groups, head_dim), bf16),
+            dma((3, E + 1)),
         ],
-        out_specs=(
-            fixed((tok_rows, model_width)),
-            fixed(by_row),
-            fixed(by_row),
-            grad_block,
-            grad_block,
-        ),
-        compiler_params=pltpu.CompilerParams(vmem_limit_bytes=60 * 1024 * 1024),
-    )(flat_t, masked, tok_grads, query_grads.reshape(by_head), key_grads.reshape(by_head))
+        compiler_params=pltpu.CompilerParams(vmem_limit_bytes=8 * 1024 * 1024),
+    )(
+        tok_grads,
+        query_grads.reshape(by_head),
+        key_grads.reshape(by_head),
+        value_grads,
+        output_grads,
+    )
     return tok_grads[None], query_grads[None], key_grads[None], value_grads, output_grads
 
 

time: 57.3 us -> 51.7 us (0.902)
  Pallas kernels: 54.9 us -> 50.9 us
  local copies, waits for them, and re-layouts: 1.41 us -> 0 us
    pallas_call x1, Pallas kernels: 6.41 us -> 3.46 us  [fused(): pl.pallas_call(finish_kernel, name='finish', out_shape=(jax.ShapeDtypeStr...]
    pallas_call x1, Pallas kernels: 48.5 us -> 47.4 us  [fused(): pl.pallas_call(functools.partial(fused_kernel, (dn, gn, jn, own_heads, qu...]
    dynamic_slice x1 -> x0, local copies, waits for them, and re-layouts: 0.7 us -> none  [fused(): lax.dynamic_slice_in_dim(route[0, :, :, 0], expert_index * own_heads, own...]
    pad x1 -> x0, local copies, waits for them, and re-layouts: 0.62 us -> none  [fused(): routes = jnp.pad(routes.T, ((0, 0), (0, 128 - 2 * own_heads)))]
where the time goes in v1:
time: 51.7 us; the launch traced here: 51.5 us
  Pallas kernels  50.9 us (98%)
  between operations  0.64 us (1%)
    pallas_call x1, Pallas kernels, fused(): pl.pallas_call(functools.partial(fused_kernel, (dn, gn, jn, own_heads, qu...  47.4 us
    pallas_call x1, Pallas kernels, fused(): pl.pallas_call(finish_kernel, name='finish', out_shape=(jax.ShapeDtypeStr...  3.46 us

profile of v1, /device:TPU:25, one launch (start us, length us, event | category | flops | bytes accessed | tf_op | source)
XLA Modules:
  0.0 51.5 jit_solution(11074129200211853784)
XLA Ops:
  0.6 47.4 %fused.1 = (bf16[8,4096]{1,0:T(8,128)(2,1)S(1)}, bf16[2,4,32,128]{3,2,1,0:T(8,128)(2,1)S(1)}, bf16[2,4,32,128]{3,2,1,0:T(8,128)(2,1)S(1)}, bf16[16,1024,128]{2,1,0:T(8,128)(2,1)S(1)}, bf16[16,1024,128]{2,1,0:T(8,128)(2,1)S(1)}) custom-call(bf16[8,4096]{1,0:T(8,128)(2,1)} %bitcast.13, bf16[8,4096]{1,0:T(8,128)(2,1)} %bitcast.14, ...), custom_call_target="tpu_custom_call" | custom-call | tf_op jit(solution)/shard_map/fused/pallas_call | solution.py:587
  48.1 3.5 %finish.1 = (bf16[8,4096]{1,0:T(8,128)(2,1)}, bf16[32,8,128]{2,1,0:T(8,128)(2,1)}, bf16[32,8,128]{2,1,0:T(8,128)(2,1)}, bf16[16,1024,128]{2,1,0:T(8,128)(2,1)}, bf16[16,1024,128]{2,1,0:T(8,128)(2,1)}) custom-call(bf16[8,4096]{1,0:T(8,128)(2,1)S(1)} %get-tuple-element.15.tok_in, bf16[8,32,128]{2,1,0:T(8,128)(2,1)S(1)} %bitcast.11, ...), custom_call_target="tpu_custom_call" | custom-call | tf_op jit(solution)/shard_map/finish/pallas_call | solution.py:655

commit v2 on v1

--- a/solution.py
+++ b/solution.py
@@ -234,17 +234,21 @@
     back,
     back_in,
     term,
+    term_side,
+    term_sum,
     term_in,
+    own_rows,
     sem_weight,
     sem_own,
-    sem_rows,
+    sem_piece,
+    sem_block,
     sem_routes,
-    sem_line,
     sem_side,
     sem_heads,
     sem_part,
     sem_factor,
     sem_back,
+    sem_half,
     sem_term,
 ):
     dn, gn, jn, own_heads, query_rows, tok_rows, width, head_dim = sizes
@@ -258,13 +262,7 @@
     def at(dd, gg, jj):
         return {"dp": lax.rem(d + dd, dn), "head": lax.rem(g + gg, gn), "expert": lax.rem(j + jj, jn)}
 
-    others = [
-        (dd, gg, jj)
-        for dd in range(dn)
-        for gg in range(gn)
-        for jj in range(jn)
-        if (dd, gg, jj) != (0, 0, 0)
-    ]
+    others = [(dd, gg) for gg in range(gn) for dd in range(dn) if (dd, gg) != (0, 0)]
     sent = []
 
     def send(src, dst, sems, slot, where):
@@ -288,54 +286,91 @@
         for i, hbm in enumerate((value_hbm, output_hbm))
     ]
     own = [
-        pltpu.make_async_copy(tok.at[:, columns(d)], rows.at[block, 0, d], sem_own.at[0]),
-        pltpu.make_async_copy(cot.at[:, columns(d)], rows.at[block, 1, d], sem_own.at[1]),
+        pltpu.make_async_copy(tok, own_rows.at[0], sem_own.at[0]),
+        pltpu.make_async_copy(cot, own_rows.at[1], sem_own.at[1]),
+        pltpu.make_async_copy(tok.at[:, columns(d)], rows.at[block, 0, d], sem_own.at[2]),
+        pltpu.make_async_copy(cot.at[:, columns(d)], rows.at[block, 1, d], sem_own.at[3]),
         pltpu.make_async_copy(
             value_routes_in.at[pl.ds(j * own_heads, own_heads)],
             routes.at[d, pl.ds(0, own_heads)],
-            sem_own.at[2],
+            sem_own.at[4],
         ),
         pltpu.make_async_copy(
             output_routes_in.at[pl.ds(j * own_heads, own_heads)],
             routes.at[d, pl.ds(own_heads, own_heads)],
-            sem_own.at[3],
-        ),
-        pltpu.make_async_copy(q_in, heads_raw.at[0], sem_own.at[4]),
-        pltpu.make_async_copy(k_in, heads_raw.at[1], sem_own.at[5]),
+            sem_own.at[5],
+        ),
+        pltpu.make_async_copy(q_in, heads_raw.at[0], sem_own.at[6]),
+        pltpu.make_async_copy(k_in, heads_raw.at[1], sem_own.at[7]),
     ]
     for copy in own:
         copy.start()
 
     barrier = pltpu.get_barrier_semaphore()
-    for where in others:
+
+    def greet(where):
         pl.semaphore_signal(
             barrier, inc=1, device_id=at(*where), device_id_type=pl.DeviceIdType.MESH
         )
-    pl.semaphore_wait(barrier, len(others))
-
-    first, late, line, side = [[], []], [], [[], []], [[], []]
-    for i in (1, 0):
-        for dd in range(1, dn):
-            target = columns(lax.rem(d + dd, dn))
-            source = (tok, cot)[i]
-            first[i].append(
-                send(source.at[:, target], rows.at[block, i, d], sem_rows, (dd, i), (dd, 0, 0))
-            )
-    for copy in weights_on_way:
-        copy.start()
+
+    for dd, gg in others:
+        greet((dd, gg, 0))
+    for jj in range(1, jn):
+        greet((0, 0, jj))
     for copy in own:
         copy.wait()
+    pl.semaphore_wait(barrier, len(others) + jn - 1)
+
+    def share(i):
+        for dd, gg in others:
+            copy = pltpu.make_async_remote_copy(
+                src_ref=own_rows.at[i, :, columns(lax.rem(d + dd, dn))],
+                dst_ref=rows.at[block, i, d],
+                send_sem=sem_piece.at[dd, gg, i],
+                recv_sem=sem_block.at[g, i],
+                device_id=at(dd, gg, 0),
+                device_id_type=pl.DeviceIdType.MESH,
+            )
+            copy.start()
+            sent.append(copy)
+
+    def side(source, jj, i):
+        block_rows = rows.at[source * jn + j, i]
+        return pltpu.make_async_remote_copy(
+            src_ref=block_rows,
+            dst_ref=block_rows,
+            send_sem=sem_side.at[0, source, jj, i],
+            recv_sem=sem_side.at[1, source, jj, i],
+            device_id=at(0, 0, jj),
+            device_id_type=pl.DeviceIdType.MESH,
+        )
+
+    def relay(i, nearest):
+        for k in range(gn):
+            order = sorted(range(gn), key=lambda t: (abs(t - k), t))
+
+            @pl.when(g == k)
+            def _(k=k, order=order):
+                for source in order[nearest]:
+                    count = dn - 1 if source == k else dn
+                    if count:
+                        came = rows.at[source * jn + j, i, pl.ds(0, count)]
+                        pltpu.make_async_remote_copy(
+                            src_ref=came,
+                            dst_ref=came,
+                            send_sem=sem_piece.at[0, 0, i],
+                            recv_sem=sem_block.at[source, i],
+                            device_id=at(0, 0, 0),
+                            device_id_type=pl.DeviceIdType.MESH,
+                        ).wait_recv()
+                    for jj in range(1, jn):
+                        side(source, jj, i).start()
+
+    near, far = slice(0, gn // 2), slice(gn // 2, gn)
+    share(1)
     late = [
         send(routes.at[d], routes.at[d], sem_routes, (dd,), (dd, 0, 0)) for dd in range(1, dn)
     ]
-    for i in (1, 0):
-        for copy in first[i]:
-            copy.wait_recv()
-        here = rows.at[block, i]
-        for gg in range(1, gn):
-            line[i].append(send(here, here, sem_line, (gg, i), (0, gg, 0)))
-        for jj in range(1, jn):
-            side[i].append(send(here, here, sem_side, (0, jj, i), (0, 0, jj)))
     for i in range(2):
         turned = jnp.transpose(heads_raw[i].astype(f32), (1, 0, 2)).astype(bf16)
         for jj in range(jn):
@@ -349,16 +384,16 @@
                 send(by_heads.at[i, peer], heads_in.at[i, j], sem_heads, (i, jj), (0, 0, jj))
             )
 
-    def forward(i):
-        for gg in range(1, gn):
-            line[i][gg - 1].wait_recv()
-            came = rows.at[lax.rem(g + gn - gg, gn) * jn + j, i]
+    for copy in weights_on_way:
+        copy.start()
+    relay(1, near)
+    share(0)
+    relay(1, far)
+
+    def flatten(i):
+        for source in range(gn):
             for jj in range(1, jn):
-                side[i].append(send(came, came, sem_side, (gg, jj, i), (0, 0, jj)))
-
-    def flatten(i):
-        for copy in side[i]:
-            copy.wait_recv()
+                side(source, jj, i).wait_recv()
         for b in range(dn):
             piece = jnp.concatenate([rows[s, i, b].astype(f32) for s in range(sources)], axis=0)
             flat[i, b * seq_len : (b + 1) * seq_len, :] = piece.astype(bf16)
@@ -396,15 +431,6 @@
             for dd in range(1, dn)
         ]
 
-    forward(1)
-    flatten(1)
-    for copy in late:
-        copy.wait_recv()
-    for b in range(dn):
-        turn_routes(b)
-    upstream_on_way = project(1)
-    forward(0)
-
     query_pos = lax.broadcasted_iota(jnp.int32, (seq_len, seq_len), 0)
     key_pos = lax.broadcasted_iota(jnp.int32, (seq_len, seq_len), 1)
     causal = key_pos <= query_pos
@@ -452,6 +478,14 @@
         top = jnp.max(jnp.where(causal, scores, -jnp.inf), axis=-1, keepdims=True)
         soft = jnp.where(causal, jnp.exp(scores - top), 0.0)
         prob_keep[h] = soft / jnp.sum(soft, axis=-1, keepdims=True)
+    for copy in late:
+        copy.wait_recv()
+    for b in range(dn):
+        turn_routes(b)
+    relay(0, near)
+    flatten(1)
+    upstream_on_way = project(1)
+    relay(0, far)
     for copy in upstream_on_way:
         copy.wait_recv()
     for h in range(own_heads):
@@ -472,17 +506,21 @@
                 [weight[0, 2 * c, n : n + step, :], weight[0, 2 * c + 1, n : n + step, :]], axis=1
             )
             added = added + across(masked[0, c], both)
-        for r in range(dn * sources):
-            term[r, :, n : n + step] = added[r * tok_rows : (r + 1) * tok_rows].astype(bf16)
-    terms = []
-    for slot, (dd, gg, jj) in enumerate(others):
-        target = (
-            lax.rem(d + dd, dn) * sources + lax.rem(g + gg, gn) * jn + lax.rem(j + jj, jn)
-        )
-        terms.append(
-            send(term.at[target], term_in.at[d * sources + block], sem_term, (slot,), (dd, gg, jj))
-        )
-    term_in[d * sources + block] = term[d * sources + block]
+        for b in range(dn):
+            for r in range(sources):
+                first = (b * sources + r) * tok_rows
+                term[r % jn, r // jn, b, :, n : n + step] = added[first : first + tok_rows].astype(
+                    bf16
+                )
+    halves = {}
+    onward = list(range(1, gn)) + [0]
+    for gg in onward:
+        target = lax.rem(g + gg, gn)
+        for jj in range(1, jn):
+            peer = lax.rem(j + jj, jn)
+            halves[gg, jj] = send(
+                term.at[peer, target], term_side.at[jj, gg], sem_half, (gg, jj), (0, 0, jj)
+            )
 
     for copy in values_on_way:
         copy.wait_recv()
@@ -513,6 +551,27 @@
             out[2 * c + 1] = whole[:, head_dim:].astype(bf16)
 
     gradients(0, vg_out)
+    terms = []
+    for gg in onward:
+        target = lax.rem(g + gg, gn)
+        whole = term[j, target].astype(f32)
+        for jj in range(1, jn):
+            halves[gg, jj].wait_recv()
+            whole = whole + term_side[jj, gg].astype(f32)
+        term_sum[gg] = whole.astype(bf16)
+        for dd in range(dn):
+            if (dd, gg) == (0, 0):
+                term_in[g, d] = term_sum[gg, d]
+            else:
+                terms.append(
+                    send(
+                        term_sum.at[gg, lax.rem(d + dd, dn)],
+                        term_in.at[g, d],
+                        sem_term,
+                        (dd, gg),
+                        (dd, gg, 0),
+                    )
+                )
     for copy in output_spread:
         copy.wait_recv()
     mask(1)
@@ -527,12 +586,16 @@
     for copy in terms:
         copy.wait_recv()
     for b in range(dn):
-        total_rows = term_in[b * sources].astype(f32)
-        for s in range(1, sources):
-            total_rows = total_rows + term_in[b * sources + s].astype(f32)
+        total_rows = term_in[0, b].astype(f32)
+        for s in range(1, gn):
+            total_rows = total_rows + term_in[s, b].astype(f32)
         tok_out[:, b * width : (b + 1) * width] = total_rows.astype(bf16)
     for copy in sent:
         copy.wait_send()
+    for source in range(gn):
+        for jj in range(1, jn):
+            for i in range(2):
+                side(source, jj, i).wait_send()
 
 
 def finish_kernel(
@@ -617,19 +680,23 @@
             pltpu.VMEM((own_heads, seq_len, head_dim), bf16),
             pltpu.VMEM((jn, 2, own_heads, query_rows, head_dim), bf16),
             pltpu.VMEM((jn, 2, own_heads, query_rows, head_dim), bf16),
-            pltpu.VMEM((dn * sources, tok_rows, width), bf16),
-            pltpu.VMEM((dn * sources, tok_rows, width), bf16),
+            pltpu.VMEM((jn, gn, dn, tok_rows, width), bf16),
+            pltpu.VMEM((jn, gn, dn, tok_rows, width), bf16),
+            pltpu.VMEM((gn, dn, tok_rows, width), bf16),
+            pltpu.VMEM((gn, dn, tok_rows, width), bf16),
+            pltpu.VMEM((2, tok_rows, model_width), bf16),
             dma((2,)),
-            dma((6,)),
-            dma((2, dn, 2)),
+            dma((8,)),
+            dma((dn, gn, 2)),
+            dma((gn, 2)),
             dma((2, dn)),
-            dma((2, gn, 2)),
             dma((2, gn, jn, 2)),
             dma((2, 2, jn)),
             dma((2, dn, 2)),
             dma((2, dn, 2)),
             dma((2, jn)),
-            dma((2, dn * sources)),
+            dma((2, gn, jn)),
+            dma((2, dn, gn)),
         ],
         compiler_params=pltpu.CompilerParams(
             collective_id=0, has_side_effects=True, vmem_limit_bytes=40 * 1024 * 1024
@@ -683,7 +750,8 @@
     groups, pairs_dev = args[2].shape[2], args[6].shape[0]
     dp_count, expert_count = lax.axis_size("dp"), lax.axis_size("expert")
     whole_heads = groups % expert_count == 0 and pairs_dev == groups // expert_count * E
-    if whole_heads and args[0].shape[2] % (dp_count * 256) == 0 and args[2].shape[1] <= 64:
+    small = args[4].shape[2] <= 128
+    if whole_heads and small and args[0].shape[2] % (dp_count * 256) == 0:
         return fused(*args)
     return local(*args)
 

time: 51.7 us -> 47.7 us (0.923)
  the two profiles are of different devices: /device:TPU:25 before, /device:TPU:0 now
where the time goes in v2:
time: 47.7 us; the launch traced here: 47.5 us
  Pallas kernels  46.9 us (98%)
  between operations  0.64 us (1%)
    pallas_call x1, Pallas kernels, fused(): pl.pallas_call(functools.partial(fused_kernel, (dn, gn, jn, own_heads, qu...  43.4 us
    pallas_call x1, Pallas kernels, fused(): pl.pallas_call(finish_kernel, name='finish', out_shape=(jax.ShapeDtypeStr...  3.46 us

profile of v2, /device:TPU:0, one launch (start us, length us, event | category | flops | bytes accessed | tf_op | source)
XLA Modules:
  0.0 47.5 jit_solution(16484734032877312119)
XLA Ops:
  0.6 43.4 %fused.1 = (bf16[8,4096]{1,0:T(8,128)(2,1)S(1)}, bf16[2,4,32,128]{3,2,1,0:T(8,128)(2,1)S(1)}, bf16[2,4,32,128]{3,2,1,0:T(8,128)(2,1)S(1)}, bf16[16,1024,128]{2,1,0:T(8,128)(2,1)S(1)}, bf16[16,1024,128]{2,1,0:T(8,128)(2,1)S(1)}) custom-call(bf16[8,4096]{1,0:T(8,128)(2,1)} %bitcast.13, bf16[8,4096]{1,0:T(8,128)(2,1)} %bitcast.14, ...), custom_call_target="tpu_custom_call" | custom-call | tf_op jit(solution)/shard_map/fused/pallas_call | solution.py:650
  44.1 3.5 %finish.1 = (bf16[8,4096]{1,0:T(8,128)(2,1)}, bf16[32,8,128]{2,1,0:T(8,128)(2,1)}, bf16[32,8,128]{2,1,0:T(8,128)(2,1)}, bf16[16,1024,128]{2,1,0:T(8,128)(2,1)}, bf16[16,1024,128]{2,1,0:T(8,128)(2,1)}) custom-call(bf16[8,4096]{1,0:T(8,128)(2,1)S(1)} %get-tuple-element.15.tok_in, bf16[8,32,128]{2,1,0:T(8,128)(2,1)S(1)} %bitcast.11, ...), custom_call_target="tpu_custom_call" | custom-call | tf_op jit(solution)/shard_map/finish/pallas_call | solution.py:722

commit v3 on v2

--- a/solution.py
+++ b/solution.py
@@ -198,6 +198,9 @@
         value_grads.astype(jnp.bfloat16),
         output_grads.astype(jnp.bfloat16),
     )
+
+
+KINDS = ("tok", "cot", "routes", "side", "heads", "part", "factor", "half", "term", "back")
 
 
 def fused_kernel(
@@ -240,21 +243,22 @@
     own_rows,
     sem_weight,
     sem_own,
-    sem_piece,
+    sem_sent,
     sem_block,
+    sem_side,
     sem_routes,
-    sem_side,
     sem_heads,
     sem_part,
     sem_factor,
     sem_back,
     sem_half,
-    sem_term,
+    sem_final,
 ):
     dn, gn, jn, own_heads, query_rows, tok_rows, width, head_dim = sizes
     sources = gn * jn
     seq_len = sources * tok_rows
     scale = head_dim ** (-0.5)
+    group = own_heads // 2 if own_heads % 2 == 0 else own_heads
     d, g, j = lax.axis_index("dp"), lax.axis_index("head"), lax.axis_index("expert")
     block = g * jn + j
     f32, bf16 = jnp.float32, jnp.bfloat16
@@ -263,20 +267,25 @@
         return {"dp": lax.rem(d + dd, dn), "head": lax.rem(g + gg, gn), "expert": lax.rem(j + jj, jn)}
 
     others = [(dd, gg) for gg in range(gn) for dd in range(dn) if (dd, gg) != (0, 0)]
-    sent = []
-
-    def send(src, dst, sems, slot, where):
-        copy = pltpu.make_async_remote_copy(
+
+    def remote(kind, src, dst, recv_sem, where):
+        return pltpu.make_async_remote_copy(
             src_ref=src,
             dst_ref=dst,
-            send_sem=sems.at[(0,) + slot],
-            recv_sem=sems.at[(1,) + slot],
-            device_id=at(*where),
+            send_sem=sem_sent.at[KINDS.index(kind)],
+            recv_sem=recv_sem,
+            device_id=where,
             device_id_type=pl.DeviceIdType.MESH,
         )
-        copy.start()
-        sent.append(copy)
-        return copy
+
+    def send(*args):
+        remote(*args).start()
+
+    def arrived(region, recv_sem):
+        remote("tok", region, region, recv_sem, at(0, 0, 0)).wait_recv()
+
+    def left(kind, region):
+        remote(kind, region, region, sem_final.at[0], at(0, 0, 0)).wait_send()
 
     def columns(index):
         return pl.ds(pl.multiple_of(index * width, 128), width)
@@ -317,83 +326,69 @@
         greet((dd, gg, 0))
     for jj in range(1, jn):
         greet((0, 0, jj))
-    for copy in own:
+    for copy in own[:2]:
         copy.wait()
     pl.semaphore_wait(barrier, len(others) + jn - 1)
 
+    def on_line(body):
+        for k in range(gn):
+            pl.when(g == k)(functools.partial(body, k))
+
+    def nearest(k):
+        return sorted(range(gn), key=lambda t: (abs(t - k), t))
+
+    def place(dd, target):
+        return {"dp": lax.rem(d + dd, dn), "head": jnp.int32(target), "expert": j}
+
     def share(i):
-        for dd, gg in others:
-            copy = pltpu.make_async_remote_copy(
-                src_ref=own_rows.at[i, :, columns(lax.rem(d + dd, dn))],
-                dst_ref=rows.at[block, i, d],
-                send_sem=sem_piece.at[dd, gg, i],
-                recv_sem=sem_block.at[g, i],
-                device_id=at(dd, gg, 0),
-                device_id_type=pl.DeviceIdType.MESH,
-            )
-            copy.start()
-            sent.append(copy)
-
-    def side(source, jj, i):
-        block_rows = rows.at[source * jn + j, i]
-        return pltpu.make_async_remote_copy(
-            src_ref=block_rows,
-            dst_ref=block_rows,
-            send_sem=sem_side.at[0, source, jj, i],
-            recv_sem=sem_side.at[1, source, jj, i],
-            device_id=at(0, 0, jj),
-            device_id_type=pl.DeviceIdType.MESH,
-        )
-
-    def relay(i, nearest):
-        for k in range(gn):
-            order = sorted(range(gn), key=lambda t: (abs(t - k), t))
-
-            @pl.when(g == k)
-            def _(k=k, order=order):
-                for source in order[nearest]:
-                    count = dn - 1 if source == k else dn
-                    if count:
-                        came = rows.at[source * jn + j, i, pl.ds(0, count)]
-                        pltpu.make_async_remote_copy(
-                            src_ref=came,
-                            dst_ref=came,
-                            send_sem=sem_piece.at[0, 0, i],
-                            recv_sem=sem_block.at[source, i],
-                            device_id=at(0, 0, 0),
-                            device_id_type=pl.DeviceIdType.MESH,
-                        ).wait_recv()
-                    for jj in range(1, jn):
-                        side(source, jj, i).start()
-
-    near, far = slice(0, gn // 2), slice(gn // 2, gn)
+        def body(k):
+            for target in nearest(k):
+                for dd in range(dn):
+                    if dd or target != k:
+                        send(
+                            ("tok", "cot")[i],
+                            own_rows.at[i, :, columns(lax.rem(d + dd, dn))],
+                            rows.at[block, i, d],
+                            sem_block.at[g, i],
+                            place(dd, target),
+                        )
+
+        on_line(body)
+
+    def relay(i, which):
+        def body(k):
+            for source in nearest(k)[which]:
+                count = dn - 1 if source == k else dn
+                here = rows.at[source * jn + j, i]
+                if count:
+                    arrived(here.at[pl.ds(0, count)], sem_block.at[source, i])
+                for jj in range(1, jn):
+                    send("side", here, here, sem_side.at[i], at(0, 0, jj))
+
+        on_line(body)
+
     share(1)
-    late = [
-        send(routes.at[d], routes.at[d], sem_routes, (dd,), (dd, 0, 0)) for dd in range(1, dn)
-    ]
+    for copy in own[2:]:
+        copy.wait()
+    for dd in range(1, dn):
+        send("routes", routes.at[d], routes.at[d], sem_routes.at[0], at(dd, 0, 0))
     for i in range(2):
         turned = jnp.transpose(heads_raw[i].astype(f32), (1, 0, 2)).astype(bf16)
         for jj in range(jn):
             by_heads[i, jj] = turned[jj * own_heads : (jj + 1) * own_heads]
         heads_in[i, j] = by_heads[i, j]
-    swapped = []
     for jj in range(1, jn):
         peer = lax.rem(j + jj, jn)
         for i in range(2):
-            swapped.append(
-                send(by_heads.at[i, peer], heads_in.at[i, j], sem_heads, (i, jj), (0, 0, jj))
-            )
-
+            send("heads", by_heads.at[i, peer], heads_in.at[i, j], sem_heads.at[0], at(0, 0, jj))
     for copy in weights_on_way:
         copy.start()
-    relay(1, near)
+    relay(1, slice(0, gn - 1))
     share(0)
-    relay(1, far)
+    relay(1, slice(gn - 1, gn))
 
     def flatten(i):
-        for source in range(gn):
-            for jj in range(1, jn):
-                side(source, jj, i).wait_recv()
+        arrived(rows.at[pl.ds(0, gn * (jn - 1)), i], sem_side.at[i])
         for b in range(dn):
             piece = jnp.concatenate([rows[s, i, b].astype(f32) for s in range(sources)], axis=0)
             flat[i, b * seq_len : (b + 1) * seq_len, :] = piece.astype(bf16)
@@ -418,18 +413,22 @@
                 both = jnp.concatenate([weight[i, p], weight[i, p + 1]], axis=1)
                 every = jnp.dot(flat[i], both, preferred_element_type=f32)
                 for b in range(dn):
-                    own_rows = every[b * seq_len : (b + 1) * seq_len]
+                    own_part = every[b * seq_len : (b + 1) * seq_len]
                     route = column(i, h, b)
-                    picked[b] = jnp.where(route == e, own_rows[:, :head_dim], picked[b])
-                    picked[b] = jnp.where(route == e + 1, own_rows[:, head_dim:], picked[b])
+                    picked[b] = jnp.where(route == e, own_part[:, :head_dim], picked[b])
+                    picked[b] = jnp.where(route == e + 1, own_part[:, head_dim:], picked[b])
             for b in range(dn):
                 part[b, i, h] = picked[b].astype(bf16)
-        return [
-            send(
-                part.at[lax.rem(d + dd, dn), i], part_in.at[dd, i], sem_part, (dd, i), (dd, 0, 0)
-            )
-            for dd in range(1, dn)
-        ]
+            if (h + 1) % group == 0:
+                heads = pl.ds(h + 1 - group, group)
+                for dd in range(1, dn):
+                    send(
+                        "part",
+                        part.at[lax.rem(d + dd, dn), i, heads],
+                        part_in.at[dd, i, heads],
+                        sem_part.at[i],
+                        at(dd, 0, 0),
+                    )
 
     query_pos = lax.broadcasted_iota(jnp.int32, (seq_len, seq_len), 0)
     key_pos = lax.broadcasted_iota(jnp.int32, (seq_len, seq_len), 1)
@@ -465,37 +464,34 @@
                     ] = jnp.where(route == e, source, 0.0).astype(bf16)
 
     def spread(i):
-        return [
-            send(factor.at[d, i], factor.at[d, i], sem_factor, (dd, i), (dd, 0, 0))
-            for dd in range(1, dn)
-        ]
-
-    for copy in swapped:
-        copy.wait_recv()
+        for dd in range(1, dn):
+            send("factor", factor.at[d, i], factor.at[d, i], sem_factor.at[i], at(dd, 0, 0))
+
+    def others_of(region, i):
+        return region.at[pl.ds(0, dn - 1), i]
+
+    arrived(heads_in.at[:, pl.ds(0, jn - 1)], sem_heads.at[0])
     for h in range(own_heads):
         query, key = joined(0, h), joined(1, h)
         scores = across(query, key) * scale
         top = jnp.max(jnp.where(causal, scores, -jnp.inf), axis=-1, keepdims=True)
         soft = jnp.where(causal, jnp.exp(scores - top), 0.0)
         prob_keep[h] = soft / jnp.sum(soft, axis=-1, keepdims=True)
-    for copy in late:
-        copy.wait_recv()
+    arrived(routes.at[pl.ds(0, dn - 1)], sem_routes.at[0])
     for b in range(dn):
         turn_routes(b)
-    relay(0, near)
+    relay(0, slice(0, 1))
     flatten(1)
-    upstream_on_way = project(1)
-    relay(0, far)
-    for copy in upstream_on_way:
-        copy.wait_recv()
+    project(1)
+    relay(0, slice(1, gn))
+    arrived(others_of(part_in, 1), sem_part.at[1])
     for h in range(own_heads):
         upstream_keep[h] = total(1, h)
         factor[d, 0, h] = over_rows(prob_keep[h].astype(bf16), upstream_keep[h]).astype(bf16)
-    value_spread = spread(0)
+    spread(0)
     flatten(0)
-    values_on_way = project(0)
-    for copy in value_spread:
-        copy.wait_recv()
+    project(0)
+    arrived(others_of(factor, 0), sem_factor.at[0])
     mask(0)
     couples = own_heads * E // 2
     step = min(width, 256)
@@ -512,25 +508,24 @@
                 term[r % jn, r // jn, b, :, n : n + step] = added[first : first + tok_rows].astype(
                     bf16
                 )
-    halves = {}
-    onward = list(range(1, gn)) + [0]
-    for gg in onward:
-        target = lax.rem(g + gg, gn)
+    for target in range(gn):
         for jj in range(1, jn):
-            peer = lax.rem(j + jj, jn)
-            halves[gg, jj] = send(
-                term.at[peer, target], term_side.at[jj, gg], sem_half, (gg, jj), (0, 0, jj)
+            send(
+                "half",
+                term.at[lax.rem(j + jj, jn), target],
+                term_side.at[jj, target],
+                sem_half.at[target],
+                at(0, 0, jj),
             )
 
-    for copy in values_on_way:
-        copy.wait_recv()
+    arrived(others_of(part_in, 0), sem_part.at[0])
     for h in range(own_heads):
         value, upstream, probs = total(0, h), upstream_keep[h], prob_keep[h]
         output = jnp.dot(probs.astype(bf16), value, preferred_element_type=f32).astype(bf16)
         factor[d, 1, h] = output
         delta = jnp.sum(output.astype(f32) * upstream.astype(f32), axis=-1, keepdims=True)
         score_keep[h] = (probs * (across(upstream, value) - delta)).astype(bf16)
-    output_spread = spread(1)
+    spread(1)
     for h in range(own_heads):
         query, key, score = joined(0, h), joined(1, h), score_keep[h]
         query_grad = (jnp.dot(score, key, preferred_element_type=f32) * scale).astype(bf16)
@@ -538,10 +533,8 @@
         for jj in range(jn):
             back[jj, 0, h] = query_grad[jj * query_rows : (jj + 1) * query_rows]
             back[jj, 1, h] = key_grad[jj * query_rows : (jj + 1) * query_rows]
-    returned = [
-        send(back.at[lax.rem(j + jj, jn)], back_in.at[j], sem_back, (jj,), (0, 0, jj))
-        for jj in range(1, jn)
-    ]
+    for jj in range(1, jn):
+        send("back", back.at[lax.rem(j + jj, jn)], back_in.at[j], sem_back.at[0], at(0, 0, jj))
 
     def gradients(i, out):
         flat_t[i] = flat[i].T
@@ -550,72 +543,75 @@
             out[2 * c] = whole[:, :head_dim].astype(bf16)
             out[2 * c + 1] = whole[:, head_dim:].astype(bf16)
 
+
+    def join_halves(which, k):
+        for target in range(gn)[which]:
+            arrived(term_side.at[pl.ds(0, jn - 1), target], sem_half.at[target])
+            whole = term[j, target].astype(f32)
+            for jj in range(1, jn):
+                whole = whole + term_side[jj, target].astype(f32)
+            term_sum[target] = whole.astype(bf16)
+            for dd in range(dn):
+                if dd == 0 and target == k:
+                    term_in[k * dn + d] = term_sum[k, d]
+                else:
+                    send(
+                        "term",
+                        term_sum.at[target, lax.rem(d + dd, dn)],
+                        term_in.at[g * dn + d],
+                        sem_final.at[0],
+                        place(dd, target),
+                    )
+
+    on_line(functools.partial(join_halves, slice(0, 1)))
     gradients(0, vg_out)
-    terms = []
-    for gg in onward:
-        target = lax.rem(g + gg, gn)
-        whole = term[j, target].astype(f32)
-        for jj in range(1, jn):
-            halves[gg, jj].wait_recv()
-            whole = whole + term_side[jj, gg].astype(f32)
-        term_sum[gg] = whole.astype(bf16)
-        for dd in range(dn):
-            if (dd, gg) == (0, 0):
-                term_in[g, d] = term_sum[gg, d]
-            else:
-                terms.append(
-                    send(
-                        term_sum.at[gg, lax.rem(d + dd, dn)],
-                        term_in.at[g, d],
-                        sem_term,
-                        (dd, gg),
-                        (dd, gg, 0),
-                    )
-                )
-    for copy in output_spread:
-        copy.wait_recv()
+    on_line(functools.partial(join_halves, slice(1, gn)))
+    arrived(others_of(factor, 1), sem_factor.at[1])
     mask(1)
     gradients(1, og_out)
 
     back_in[j] = back[j]
-    for copy in returned:
-        copy.wait_recv()
+    arrived(back_in.at[pl.ds(0, jn - 1)], sem_back.at[0])
     for jj in range(jn):
         qg_out[jj] = back_in[jj, 0]
         kg_out[jj] = back_in[jj, 1]
-    for copy in terms:
-        copy.wait_recv()
+    all_terms = term_in.at[pl.ds(0, len(others))]
+    arrived(all_terms, sem_final.at[0])
     for b in range(dn):
-        total_rows = term_in[0, b].astype(f32)
+        total_rows = term_in[b].astype(f32)
         for s in range(1, gn):
-            total_rows = total_rows + term_in[s, b].astype(f32)
+            total_rows = total_rows + term_in[s * dn + b].astype(f32)
         tok_out[:, b * width : (b + 1) * width] = total_rows.astype(bf16)
-    for copy in sent:
-        copy.wait_send()
-    for source in range(gn):
-        for jj in range(1, jn):
-            for i in range(2):
-                side(source, jj, i).wait_send()
+    for kind in ("tok", "cot", "term"):
+        left(kind, all_terms)
+    left("routes", routes.at[pl.ds(0, dn - 1)])
+    left("side", rows.at[pl.ds(0, gn * (jn - 1))])
+    left("heads", heads_in.at[:, pl.ds(0, jn - 1)])
+    left("part", part_in.at[pl.ds(0, dn - 1)])
+    left("factor", factor.at[pl.ds(0, dn - 1)])
+    left("half", term_side.at[pl.ds(0, jn - 1)])
+    left("back", back_in.at[pl.ds(0, jn - 1)])
 
 
 def finish_kernel(
     tok_in, qg_in, kg_in, vg_in, og_in, tok_out, qg_out, kg_out, vg_out, og_out, turned, sems
 ):
-    pieces = sems.shape[1]
-    size = vg_in.shape[0] // (pieces - 1)
-    copies = [pltpu.make_async_copy(tok_in, tok_out, sems.at[0, pieces - 1])]
+    pieces = E
+    size = vg_in.shape[0] // pieces
+    whole = [
+        pltpu.make_async_copy(source, out, sems.at[i])
+        for i, (source, out) in enumerate(((vg_in, vg_out), (og_in, og_out), (tok_in, tok_out)))
+    ]
     for i, (source, out) in enumerate(((vg_in, vg_out), (og_in, og_out))):
-        for n in range(pieces - 1):
+        for n in range(pieces):
             part = pl.ds(n * size, size)
-            copies.append(pltpu.make_async_copy(source.at[part], out.at[part], sems.at[i, n]))
-    for copy in copies:
-        copy.start()
-    late = []
+            pltpu.make_async_copy(source.at[part], out.at[part], sems.at[i]).start()
+    whole[2].start()
     for i, (source, out) in enumerate(((qg_in, qg_out), (kg_in, kg_out))):
         turned[i] = jnp.transpose(source[...].astype(jnp.float32), (1, 0, 2)).astype(out.dtype)
-        late.append(pltpu.make_async_copy(turned.at[i], out, sems.at[2, i]))
-        late[i].start()
-    for copy in copies + late:
+        whole.append(pltpu.make_async_copy(turned.at[i], out, sems.at[3 + i]))
+        whole[3 + i].start()
+    for copy in whole:
         copy.wait()
 
 
@@ -683,20 +679,20 @@
             pltpu.VMEM((jn, gn, dn, tok_rows, width), bf16),
             pltpu.VMEM((jn, gn, dn, tok_rows, width), bf16),
             pltpu.VMEM((gn, dn, tok_rows, width), bf16),
-            pltpu.VMEM((gn, dn, tok_rows, width), bf16),
+            pltpu.VMEM((gn * dn, tok_rows, width), bf16),
             pltpu.VMEM((2, tok_rows, model_width), bf16),
             dma((2,)),
             dma((8,)),
-            dma((dn, gn, 2)),
+            dma((len(KINDS),)),
             dma((gn, 2)),
-            dma((2, dn)),
-            dma((2, gn, jn, 2)),
-            dma((2, 2, jn)),
-            dma((2, dn, 2)),
-            dma((2, dn, 2)),
-            dma((2, jn)),
-            dma((2, gn, jn)),
-            dma((2, dn, gn)),
+            dma((2,)),
+            dma((1,)),
+            dma((1,)),
+            dma((2,)),
+            dma((2,)),
+            dma((1,)),
+            dma((gn,)),
+            dma((1,)),
         ],
         compiler_params=pltpu.CompilerParams(
             collective_id=0, has_side_effects=True, vmem_limit_bytes=40 * 1024 * 1024
@@ -733,7 +729,7 @@
         out_specs=(hbm,) * 5,
         scratch_shapes=[
             pltpu.VMEM((2, query_rows, groups, head_dim), bf16),
-            dma((3, E + 1)),
+            dma((5,)),
         ],
         compiler_params=pltpu.CompilerParams(vmem_limit_bytes=8 * 1024 * 1024),
     )(
@@ -751,7 +747,7 @@
     dp_count, expert_count = lax.axis_size("dp"), lax.axis_size("expert")
     whole_heads = groups % expert_count == 0 and pairs_dev == groups // expert_count * E
     small = args[4].shape[2] <= 128
-    if whole_heads and small and args[0].shape[2] % (dp_count * 256) == 0:
+    if whole_heads and small and expert_count > 1 and dp_count > 1 and args[0].shape[2] % (dp_count * 256) == 0:
         return fused(*args)
     return local(*args)
 

time: 47.7 us -> 45 us (0.943)
  the two profiles are of different devices: /device:TPU:0 before, /device:TPU:1 now
where the time goes in v3:
time: 45 us; the launch traced here: 44.9 us
  Pallas kernels  44.2 us (98%)
  between operations  0.64 us (1%)
    pallas_call x1, Pallas kernels, fused(): pl.pallas_call(functools.partial(fused_kernel, (dn, gn, jn, own_heads, qu...  40.9 us
    pallas_call x1, Pallas kernels, fused(): pl.pallas_call(finish_kernel, name='finish', out_shape=(jax.ShapeDtypeStr...  3.36 us

profile of v3, /device:TPU:1, one launch (start us, length us, event | category | flops | bytes accessed | tf_op | source)
XLA Modules:
  0.0 44.9 jit_solution(18033799550034465866)
XLA Ops:
  0.6 40.9 %fused.1 = (bf16[8,4096]{1,0:T(8,128)(2,1)S(1)}, bf16[2,4,32,128]{3,2,1,0:T(8,128)(2,1)S(1)}, bf16[2,4,32,128]{3,2,1,0:T(8,128)(2,1)S(1)}, bf16[16,1024,128]{2,1,0:T(8,128)(2,1)S(1)}, bf16[16,1024,128]{2,1,0:T(8,128)(2,1)S(1)}) custom-call(bf16[8,4096]{1,0:T(8,128)(2,1)} %bitcast.13, bf16[8,4096]{1,0:T(8,128)(2,1)} %bitcast.14, ...), custom_call_target="tpu_custom_call" | custom-call | tf_op jit(solution)/shard_map/fused/pallas_call | solution.py:646
  41.5 3.4 %finish.1 = (bf16[8,4096]{1,0:T(8,128)(2,1)}, bf16[32,8,128]{2,1,0:T(8,128)(2,1)}, bf16[32,8,128]{2,1,0:T(8,128)(2,1)}, bf16[16,1024,128]{2,1,0:T(8,128)(2,1)}, bf16[16,1024,128]{2,1,0:T(8,128)(2,1)}) custom-call(bf16[8,4096]{1,0:T(8,128)(2,1)S(1)} %get-tuple-element.15.tok_in, bf16[8,32,128]{2,1,0:T(8,128)(2,1)S(1)} %bitcast.11, ...), custom_call_target="tpu_custom_call" | custom-call | tf_op jit(solution)/shard_map/finish/pallas_call | solution.py:718

commit v4 on v3

--- a/solution.py
+++ b/solution.py
@@ -200,7 +200,34 @@
     )
 
 
-KINDS = ("tok", "cot", "routes", "side", "heads", "part", "factor", "half", "term", "back")
+def line_plan(gn):
+    order = [sorted(range(gn), key=lambda t: (abs(t - k), t)) for k in range(gn)]
+    plain = (order, [row[1:] for row in order], [{} for _ in range(gn)])
+    if gn != 4:
+        return plain, plain
+    passed = (
+        [[0, 1, 3, 2], [1, 2, 0, 3], [2, 1, 3, 0], [3, 2, 0, 1]],
+        [[1, 2, 3], [2, 0], [1, 3], [2, 1, 0]],
+        [{}, {2: 0}, {1: 3}, {}],
+    )
+    return plain, passed
+
+
+KINDS = (
+    "tok",
+    "cot",
+    "onward",
+    "routes",
+    "side",
+    "heads",
+    "part",
+    "factor",
+    "cols",
+    "half",
+    "term",
+    "back",
+)
+NEAR = 2
 
 
 def fused_kernel(
@@ -219,7 +246,9 @@
     vg_out,
     og_out,
     rows,
+    far_rows,
     flat,
+    cols,
     flat_t,
     heads_raw,
     by_heads,
@@ -250,23 +279,33 @@
     sem_heads,
     sem_part,
     sem_factor,
+    sem_cols,
     sem_back,
     sem_half,
     sem_final,
 ):
     dn, gn, jn, own_heads, query_rows, tok_rows, width, head_dim = sizes
     sources = gn * jn
+    cn, xn = NEAR, dn // NEAR
     seq_len = sources * tok_rows
     scale = head_dim ** (-0.5)
     group = own_heads // 2 if own_heads % 2 == 0 else own_heads
     d, g, j = lax.axis_index("dp"), lax.axis_index("head"), lax.axis_index("expert")
     block = g * jn + j
+    x, c = d // cn, lax.rem(d, cn)
     f32, bf16 = jnp.float32, jnp.bfloat16
 
     def at(dd, gg, jj):
         return {"dp": lax.rem(d + dd, dn), "head": lax.rem(g + gg, gn), "expert": lax.rem(j + jj, jn)}
 
-    others = [(dd, gg) for gg in range(gn) for dd in range(dn) if (dd, gg) != (0, 0)]
+    def near(cc):
+        return lax.rem(c + cc, cn)
+
+    others = [(cc, gg) for gg in range(gn) for cc in range(cn) if (cc, gg) != (0, 0)]
+    afar = [(xx, cc) for xx in range(1, xn) for cc in range(cn)]
+
+    def across(xx, cc):
+        return {"dp": lax.rem(x + xx, xn) * cn + near(cc), "head": g, "expert": j}
 
     def remote(kind, src, dst, recv_sem, where):
         return pltpu.make_async_remote_copy(
@@ -291,26 +330,34 @@
         return pl.ds(pl.multiple_of(index * width, 128), width)
 
     weights_on_way = [
-        pltpu.make_async_copy(hbm.at[:, columns(d), :], weight.at[i], sem_weight.at[i])
-        for i, hbm in enumerate((value_hbm, output_hbm))
+        pltpu.make_async_copy(
+            hbm.at[:, columns(q * cn + c), :], weight.at[i, :, q], sem_weight.at[i, q]
+        )
+        for i, hbm in ((1, output_hbm), (0, value_hbm))
+        for q in range(xn)
     ]
     own = [
         pltpu.make_async_copy(tok, own_rows.at[0], sem_own.at[0]),
         pltpu.make_async_copy(cot, own_rows.at[1], sem_own.at[1]),
-        pltpu.make_async_copy(tok.at[:, columns(d)], rows.at[block, 0, d], sem_own.at[2]),
-        pltpu.make_async_copy(cot.at[:, columns(d)], rows.at[block, 1, d], sem_own.at[3]),
         pltpu.make_async_copy(
             value_routes_in.at[pl.ds(j * own_heads, own_heads)],
             routes.at[d, pl.ds(0, own_heads)],
-            sem_own.at[4],
+            sem_own.at[2],
         ),
         pltpu.make_async_copy(
             output_routes_in.at[pl.ds(j * own_heads, own_heads)],
             routes.at[d, pl.ds(own_heads, own_heads)],
-            sem_own.at[5],
+            sem_own.at[3],
         ),
-        pltpu.make_async_copy(q_in, heads_raw.at[0], sem_own.at[6]),
-        pltpu.make_async_copy(k_in, heads_raw.at[1], sem_own.at[7]),
+        pltpu.make_async_copy(q_in, heads_raw.at[0], sem_own.at[4]),
+        pltpu.make_async_copy(k_in, heads_raw.at[1], sem_own.at[5]),
+    ]
+    own += [
+        pltpu.make_async_copy(
+            source.at[:, columns(q * cn + c)], rows.at[block, i, c, q], sem_own.at[6 + i * xn + q]
+        )
+        for i, source in enumerate((tok, cot))
+        for q in range(xn)
     ]
     for copy in own:
         copy.start()
@@ -319,51 +366,67 @@
 
     def greet(where):
         pl.semaphore_signal(
-            barrier, inc=1, device_id=at(*where), device_id_type=pl.DeviceIdType.MESH
+            barrier, inc=1, device_id=where, device_id_type=pl.DeviceIdType.MESH
         )
 
-    for dd, gg in others:
-        greet((dd, gg, 0))
+    for cc, gg in others:
+        greet({"dp": x * cn + near(cc), "head": lax.rem(g + gg, gn), "expert": j})
+    for xx, cc in afar:
+        greet(across(xx, cc))
     for jj in range(1, jn):
-        greet((0, 0, jj))
+        greet(at(0, 0, jj))
     for copy in own[:2]:
         copy.wait()
-    pl.semaphore_wait(barrier, len(others) + jn - 1)
+    pl.semaphore_wait(barrier, len(others) + len(afar) + jn - 1)
 
     def on_line(body):
         for k in range(gn):
             pl.when(g == k)(functools.partial(body, k))
 
-    def nearest(k):
-        return sorted(range(gn), key=lambda t: (abs(t - k), t))
-
-    def place(dd, target):
-        return {"dp": lax.rem(d + dd, dn), "head": jnp.int32(target), "expert": j}
+    plans = line_plan(gn)
+
+    def place(cc, target):
+        return {"dp": x * cn + near(cc), "head": jnp.int32(target), "expert": j}
 
     def share(i):
         def body(k):
-            for target in nearest(k):
-                for dd in range(dn):
-                    if dd or target != k:
-                        send(
-                            ("tok", "cot")[i],
-                            own_rows.at[i, :, columns(lax.rem(d + dd, dn))],
-                            rows.at[block, i, d],
-                            sem_block.at[g, i],
-                            place(dd, target),
-                        )
+            for target in [k] + plans[i][1][k]:
+                for cc in range(cn):
+                    for q in range(xn):
+                        if cc or target != k:
+                            send(
+                                ("tok", "cot")[i],
+                                own_rows.at[i, :, columns(q * cn + near(cc))],
+                                rows.at[block, i, c, q],
+                                sem_block.at[g, i],
+                                place(cc, target),
+                            )
 
         on_line(body)
+
+    def exchange(i, source):
+        for xx in range(1, xn):
+            send(
+                "cols",
+                rows.at[source, i, :, lax.rem(x + xx, xn)],
+                far_rows.at[source, i, x],
+                sem_cols.at[i],
+                across(xx, 0),
+            )
 
     def relay(i, which):
         def body(k):
-            for source in nearest(k)[which]:
-                count = dn - 1 if source == k else dn
+            for source in plans[i][0][k][which]:
+                count = cn - 1 if source == k else cn
                 here = rows.at[source * jn + j, i]
                 if count:
                     arrived(here.at[pl.ds(0, count)], sem_block.at[source, i])
+                onward = plans[i][2][k]
+                if source in onward:
+                    send("onward", here, here, sem_block.at[source, i], place(0, onward[source]))
                 for jj in range(1, jn):
-                    send("side", here, here, sem_side.at[i], at(0, 0, jj))
+                    send("side", here, here, sem_side.at[source, i], at(0, 0, jj))
+                exchange(i, source * jn + j)
 
         on_line(body)
 
@@ -383,15 +446,41 @@
             send("heads", by_heads.at[i, peer], heads_in.at[i, j], sem_heads.at[0], at(0, 0, jj))
     for copy in weights_on_way:
         copy.start()
-    relay(1, slice(0, gn - 1))
+    relay(1, slice(0, 2))
     share(0)
-    relay(1, slice(gn - 1, gn))
+    relay(0, slice(0, 1))
+    relay(1, slice(2, gn))
 
     def flatten(i):
-        arrived(rows.at[pl.ds(0, gn * (jn - 1)), i], sem_side.at[i])
-        for b in range(dn):
-            piece = jnp.concatenate([rows[s, i, b].astype(f32) for s in range(sources)], axis=0)
-            flat[i, b * seq_len : (b + 1) * seq_len, :] = piece.astype(bf16)
+        for b in range(cn):
+            for q in range(xn):
+                piece = jnp.concatenate(
+                    [rows[s, i, b, q].astype(f32) for s in range(sources)], axis=0
+                )
+                flat[i, q, b * seq_len : (b + 1) * seq_len, :] = piece.astype(bf16)
+
+    def own_span(place_x):
+        return pl.ds(pl.multiple_of(place_x * cn * seq_len, cn * seq_len), cn * seq_len)
+
+    def from_side(i, which):
+        def body(k):
+            for source in plans[i][0][k][which]:
+                arrived(rows.at[pl.ds(0, jn - 1), i], sem_side.at[source, i])
+                for jj in range(1, jn):
+                    exchange(i, source * jn + lax.rem(j + jj, jn))
+
+        on_line(body)
+
+    def gather_columns(i):
+        arrived(far_rows.at[:, i, pl.ds(0, xn - 1)], sem_cols.at[i])
+        cols[i, own_span(x), :] = flat[i, x]
+        for xx in range(1, xn):
+            other = lax.rem(x + xx, xn)
+            pieces = [
+                far_rows[s, i, other, b].astype(f32) for b in range(cn) for s in range(sources)
+            ]
+            cols[i, own_span(other), :] = jnp.concatenate(pieces, axis=0).astype(bf16)
+        flat_t[i] = cols[i].T
 
     def column(i, h, b):
         c = i * own_heads + h
@@ -405,30 +494,34 @@
         route_columns[b] = lines.T
 
     def project(i):
-        weights_on_way[i].wait()
         for h in range(own_heads):
-            picked = [jnp.zeros((seq_len, head_dim), f32) for _ in range(dn)]
+            picked = [jnp.zeros((seq_len, head_dim), f32) for _ in range(cn)]
             for e in range(0, E, 2):
                 p = h * E + e
-                both = jnp.concatenate([weight[i, p], weight[i, p + 1]], axis=1)
-                every = jnp.dot(flat[i], both, preferred_element_type=f32)
-                for b in range(dn):
+                every = jnp.zeros((cn * seq_len, 2 * head_dim), f32)
+                for q in range(xn):
+                    both = jnp.concatenate([weight[i, p, q], weight[i, p + 1, q]], axis=1)
+                    every = every + jnp.dot(flat[i, q], both, preferred_element_type=f32)
+                for b in range(cn):
                     own_part = every[b * seq_len : (b + 1) * seq_len]
-                    route = column(i, h, b)
+                    route = column(i, h, x * cn + b)
                     picked[b] = jnp.where(route == e, own_part[:, :head_dim], picked[b])
                     picked[b] = jnp.where(route == e + 1, own_part[:, head_dim:], picked[b])
-            for b in range(dn):
+            for b in range(cn):
                 part[b, i, h] = picked[b].astype(bf16)
             if (h + 1) % group == 0:
                 heads = pl.ds(h + 1 - group, group)
-                for dd in range(1, dn):
+                for cc in range(1, cn):
                     send(
                         "part",
-                        part.at[lax.rem(d + dd, dn), i, heads],
-                        part_in.at[dd, i, heads],
+                        part.at[near(cc), i, heads],
+                        part_in.at[cc, i, heads],
                         sem_part.at[i],
-                        at(dd, 0, 0),
+                        place_near(cc),
                     )
+
+    def place_near(cc):
+        return {"dp": x * cn + near(cc), "head": g, "expert": j}
 
     query_pos = lax.broadcasted_iota(jnp.int32, (seq_len, seq_len), 0)
     key_pos = lax.broadcasted_iota(jnp.int32, (seq_len, seq_len), 1)
@@ -438,76 +531,93 @@
         return jnp.concatenate([heads_in[i, jj, h] for jj in range(jn)], axis=0)
 
     def total(i, h):
-        whole = part[d, i, h].astype(f32)
-        for dd in range(1, dn):
-            whole = whole + part_in[dd, i, h].astype(f32)
+        whole = part[c, i, h].astype(f32)
+        for cc in range(1, cn):
+            whole = whole + part_in[cc, i, h].astype(f32)
         return whole.astype(bf16)
 
-    def across(a, b):
+    def across_rows(a, b):
         return lax.dot_general(a, b, (((1,), (1,)), ((), ())), preferred_element_type=f32)
 
     def over_rows(a, b):
         return lax.dot_general(a, b, (((0,), (0,)), ((), ())), preferred_element_type=f32)
 
-    def mask(i):
-        for h in range(own_heads):
-            for b in range(dn):
-                source = factor[b, i, h].astype(f32)
-                route = column(i, h, b)
-                for e in range(E):
-                    p = h * E + e
-                    masked[
-                        i,
-                        p // 2,
-                        b * seq_len : (b + 1) * seq_len,
-                        (p % 2) * head_dim : (p % 2 + 1) * head_dim,
-                    ] = jnp.where(route == e, source, 0.0).astype(bf16)
+    def mask(i, groups_x):
+        for xx in groups_x:
+            for h in range(own_heads):
+                for cc in range(cn):
+                    b = lax.rem(x + xx, xn) * cn + cc
+                    source = factor[b, i, h].astype(f32)
+                    route = column(i, h, b)
+                    line = pl.ds(pl.multiple_of(b * seq_len, seq_len), seq_len)
+                    for e in range(E):
+                        p = h * E + e
+                        masked[
+                            i, p // 2, line, (p % 2) * head_dim : (p % 2 + 1) * head_dim
+                        ] = jnp.where(route == e, source, 0.0).astype(bf16)
 
     def spread(i):
-        for dd in range(1, dn):
-            send("factor", factor.at[d, i], factor.at[d, i], sem_factor.at[i], at(dd, 0, 0))
-
-    def others_of(region, i):
-        return region.at[pl.ds(0, dn - 1), i]
+        for cc in range(1, cn):
+            send("factor", factor.at[d, i], factor.at[d, i], sem_factor.at[i, 0], place_near(cc))
+        for xx in range(1, xn):
+            send("factor", factor.at[d, i], factor.at[d, i], sem_factor.at[i, 1], across(xx, 0))
+
+    def near_factor(i):
+        arrived(factor.at[pl.ds(0, cn - 1), i], sem_factor.at[i, 0])
+
+    def hand_over(i):
+        arrived(factor.at[pl.ds(0, xn - 1), i], sem_factor.at[i, 1])
+        for xx in range(1, xn):
+            came = factor.at[lax.rem(x + xx, xn) * cn + c, i]
+            for cc in range(1, cn):
+                send("factor", came, came, sem_factor.at[i, 2], place_near(cc))
+
+    def far_factor(i):
+        arrived(factor.at[pl.ds(0, (xn - 1) * (cn - 1)), i], sem_factor.at[i, 2])
 
     arrived(heads_in.at[:, pl.ds(0, jn - 1)], sem_heads.at[0])
     for h in range(own_heads):
         query, key = joined(0, h), joined(1, h)
-        scores = across(query, key) * scale
+        scores = across_rows(query, key) * scale
         top = jnp.max(jnp.where(causal, scores, -jnp.inf), axis=-1, keepdims=True)
         soft = jnp.where(causal, jnp.exp(scores - top), 0.0)
         prob_keep[h] = soft / jnp.sum(soft, axis=-1, keepdims=True)
     arrived(routes.at[pl.ds(0, dn - 1)], sem_routes.at[0])
     for b in range(dn):
         turn_routes(b)
-    relay(0, slice(0, 1))
+    from_side(1, slice(0, gn))
     flatten(1)
+    relay(0, slice(1, 2))
+    for copy in weights_on_way[:xn]:
+        copy.wait()
     project(1)
-    relay(0, slice(1, gn))
-    arrived(others_of(part_in, 1), sem_part.at[1])
+    relay(0, slice(2, gn))
+    arrived(part_in.at[pl.ds(0, cn - 1), 1], sem_part.at[1])
     for h in range(own_heads):
         upstream_keep[h] = total(1, h)
         factor[d, 0, h] = over_rows(prob_keep[h].astype(bf16), upstream_keep[h]).astype(bf16)
     spread(0)
-    flatten(0)
-    project(0)
-    arrived(others_of(factor, 0), sem_factor.at[0])
-    mask(0)
+    near_factor(0)
+    mask(0, range(0, 1))
+    for copy in weights_on_way[xn:]:
+        copy.wait()
     couples = own_heads * E // 2
     step = min(width, 256)
-    for n in range(0, width, step):
-        added = jnp.zeros((dn * seq_len, step), f32)
-        for c in range(couples):
-            both = jnp.concatenate(
-                [weight[0, 2 * c, n : n + step, :], weight[0, 2 * c + 1, n : n + step, :]], axis=1
-            )
-            added = added + across(masked[0, c], both)
-        for b in range(dn):
-            for r in range(sources):
-                first = (b * sources + r) * tok_rows
-                term[r % jn, r // jn, b, :, n : n + step] = added[first : first + tok_rows].astype(
-                    bf16
+    for q in range(xn):
+        for n in range(0, width, step):
+            added = jnp.zeros((cn * seq_len, step), f32)
+            for m in range(couples):
+                both = jnp.concatenate(
+                    [weight[0, 2 * m, q, n : n + step, :], weight[0, 2 * m + 1, q, n : n + step, :]],
+                    axis=1,
                 )
+                added = added + across_rows(masked[0, m, own_span(x), :], both)
+            for b in range(cn):
+                for r in range(sources):
+                    first = b * seq_len + r * tok_rows
+                    term[r % jn, r // jn, b, q, :, n : n + step] = added[
+                        first : first + tok_rows
+                    ].astype(bf16)
     for target in range(gn):
         for jj in range(1, jn):
             send(
@@ -518,14 +628,37 @@
                 at(0, 0, jj),
             )
 
-    arrived(others_of(part_in, 0), sem_part.at[0])
+    def join_halves(which, k):
+        for target in range(gn)[which]:
+            arrived(term_side.at[pl.ds(0, jn - 1), target], sem_half.at[target])
+            whole = term[j, target].astype(f32)
+            for jj in range(1, jn):
+                whole = whole + term_side[jj, target].astype(f32)
+            term_sum[target] = whole.astype(bf16)
+            for cc in range(cn):
+                if cc == 0 and target == k:
+                    term_in[k * cn + c] = term_sum[k, c]
+                else:
+                    send(
+                        "term",
+                        term_sum.at[target, near(cc)],
+                        term_in.at[g * cn + c],
+                        sem_final.at[0],
+                        place(cc, target),
+                    )
+
+    from_side(0, slice(0, gn))
+    flatten(0)
+    project(0)
+    arrived(part_in.at[pl.ds(0, cn - 1), 0], sem_part.at[0])
     for h in range(own_heads):
         value, upstream, probs = total(0, h), upstream_keep[h], prob_keep[h]
         output = jnp.dot(probs.astype(bf16), value, preferred_element_type=f32).astype(bf16)
         factor[d, 1, h] = output
         delta = jnp.sum(output.astype(f32) * upstream.astype(f32), axis=-1, keepdims=True)
-        score_keep[h] = (probs * (across(upstream, value) - delta)).astype(bf16)
+        score_keep[h] = (probs * (across_rows(upstream, value) - delta)).astype(bf16)
     spread(1)
+    on_line(functools.partial(join_halves, slice(0, 1)))
     for h in range(own_heads):
         query, key, score = joined(0, h), joined(1, h), score_keep[h]
         query_grad = (jnp.dot(score, key, preferred_element_type=f32) * scale).astype(bf16)
@@ -537,37 +670,26 @@
         send("back", back.at[lax.rem(j + jj, jn)], back_in.at[j], sem_back.at[0], at(0, 0, jj))
 
     def gradients(i, out):
-        flat_t[i] = flat[i].T
-        for c in range(couples):
-            whole = jnp.dot(flat_t[i], masked[i, c], preferred_element_type=f32)
-            out[2 * c] = whole[:, :head_dim].astype(bf16)
-            out[2 * c + 1] = whole[:, head_dim:].astype(bf16)
-
-
-    def join_halves(which, k):
-        for target in range(gn)[which]:
-            arrived(term_side.at[pl.ds(0, jn - 1), target], sem_half.at[target])
-            whole = term[j, target].astype(f32)
-            for jj in range(1, jn):
-                whole = whole + term_side[jj, target].astype(f32)
-            term_sum[target] = whole.astype(bf16)
-            for dd in range(dn):
-                if dd == 0 and target == k:
-                    term_in[k * dn + d] = term_sum[k, d]
-                else:
-                    send(
-                        "term",
-                        term_sum.at[target, lax.rem(d + dd, dn)],
-                        term_in.at[g * dn + d],
-                        sem_final.at[0],
-                        place(dd, target),
-                    )
-
-    on_line(functools.partial(join_halves, slice(0, 1)))
+        for m in range(couples):
+            whole = jnp.dot(flat_t[i], masked[i, m], preferred_element_type=f32)
+            out[2 * m] = whole[:, :head_dim].astype(bf16)
+            out[2 * m + 1] = whole[:, head_dim:].astype(bf16)
+
+
+    hand_over(0)
+    on_line(functools.partial(join_halves, slice(1, 2)))
+    far_factor(0)
+    mask(0, range(1, xn))
+    on_line(functools.partial(join_halves, slice(2, gn - 1)))
+    gather_columns(0)
+    hand_over(1)
+    on_line(functools.partial(join_halves, slice(gn - 1, gn)))
     gradients(0, vg_out)
-    on_line(functools.partial(join_halves, slice(1, gn)))
-    arrived(others_of(factor, 1), sem_factor.at[1])
-    mask(1)
+    near_factor(1)
+    mask(1, range(0, 1))
+    gather_columns(1)
+    far_factor(1)
+    mask(1, range(1, xn))
     gradients(1, og_out)
 
     back_in[j] = back[j]
@@ -577,17 +699,28 @@
         kg_out[jj] = back_in[jj, 1]
     all_terms = term_in.at[pl.ds(0, len(others))]
     arrived(all_terms, sem_final.at[0])
-    for b in range(dn):
-        total_rows = term_in[b].astype(f32)
-        for s in range(1, gn):
-            total_rows = total_rows + term_in[s * dn + b].astype(f32)
-        tok_out[:, b * width : (b + 1) * width] = total_rows.astype(bf16)
-    for kind in ("tok", "cot", "term"):
-        left(kind, all_terms)
+    for b in range(cn):
+        for q in range(xn):
+            total_rows = term_in[b, q].astype(f32)
+            for s in range(1, gn):
+                total_rows = total_rows + term_in[s * cn + b, q].astype(f32)
+            n = (q * cn + b) * width
+            tok_out[:, n : n + width] = total_rows.astype(bf16)
+    left("term", all_terms)
+
+    def left_line(k):
+        for i, kind in enumerate(("tok", "cot")):
+            left(kind, term_in.at[pl.ds(0, cn - 1 + cn * len(plans[i][1][k]))])
+        count = sum(len(plan[2][k]) for plan in plans)
+        if count:
+            left("onward", rows.at[pl.ds(0, count), 0])
+
+    on_line(left_line)
     left("routes", routes.at[pl.ds(0, dn - 1)])
     left("side", rows.at[pl.ds(0, gn * (jn - 1))])
     left("heads", heads_in.at[:, pl.ds(0, jn - 1)])
-    left("part", part_in.at[pl.ds(0, dn - 1)])
+    left("part", part_in.at[pl.ds(0, cn - 1)])
+    left("cols", far_rows.at[:, :, pl.ds(0, xn - 1)])
     left("factor", factor.at[pl.ds(0, dn - 1)])
     left("half", term_side.at[pl.ds(0, jn - 1)])
     left("back", back_in.at[pl.ds(0, jn - 1)])
@@ -633,6 +766,7 @@
     pairs_dev = value_experts.shape[0]
     own_heads = groups // jn
     sources = gn * jn
+    xn = dn // NEAR
     bf16 = jnp.bfloat16
 
     value_lines = value_routes.reshape(groups, 1, seq_len)
@@ -658,17 +792,19 @@
         in_specs=[hbm] * 8,
         out_specs=(vmem,) * 5,
         scratch_shapes=[
-            pltpu.VMEM((sources, 2, dn, tok_rows, width), bf16),
+            pltpu.VMEM((sources, 2, NEAR, xn, tok_rows, width), bf16),
+            pltpu.VMEM((sources, 2, xn, NEAR, tok_rows, width), bf16),
+            pltpu.VMEM((2, xn, NEAR * seq_len, width), bf16),
             pltpu.VMEM((2, dn * seq_len, width), bf16),
             pltpu.VMEM((2, width, dn * seq_len), bf16),
             pltpu.VMEM((2, query_rows, groups, head_dim), bf16),
             pltpu.VMEM((2, jn, own_heads, query_rows, head_dim), bf16),
             pltpu.VMEM((dn, 2 * own_heads, 1, seq_len), jnp.int32),
             pltpu.VMEM((dn, -(-seq_len // 128) * 128, 2 * own_heads), jnp.int32),
-            pltpu.VMEM((2, pairs_dev, width, head_dim), bf16),
+            pltpu.VMEM((2, pairs_dev, xn, width, head_dim), bf16),
             pltpu.VMEM((2, jn, own_heads, query_rows, head_dim), bf16),
-            pltpu.VMEM((dn, 2, own_heads, seq_len, head_dim), bf16),
-            pltpu.VMEM((dn, 2, own_heads, seq_len, head_dim), bf16),
+            pltpu.VMEM((NEAR, 2, own_heads, seq_len, head_dim), bf16),
+            pltpu.VMEM((NEAR, 2, own_heads, seq_len, head_dim), bf16),
             pltpu.VMEM((dn, 2, own_heads, seq_len, head_dim), bf16),
             pltpu.VMEM((2, pairs_dev // 2, dn * seq_len, 2 * head_dim), bf16),
             pltpu.VMEM((own_heads, seq_len, seq_len), bf16),
@@ -676,26 +812,27 @@
             pltpu.VMEM((own_heads, seq_len, head_dim), bf16),
             pltpu.VMEM((jn, 2, own_heads, query_rows, head_dim), bf16),
             pltpu.VMEM((jn, 2, own_heads, query_rows, head_dim), bf16),
-            pltpu.VMEM((jn, gn, dn, tok_rows, width), bf16),
-            pltpu.VMEM((jn, gn, dn, tok_rows, width), bf16),
-            pltpu.VMEM((gn, dn, tok_rows, width), bf16),
-            pltpu.VMEM((gn * dn, tok_rows, width), bf16),
+            pltpu.VMEM((jn, gn, NEAR, xn, tok_rows, width), bf16),
+            pltpu.VMEM((jn, gn, NEAR, xn, tok_rows, width), bf16),
+            pltpu.VMEM((gn, NEAR, xn, tok_rows, width), bf16),
+            pltpu.VMEM((gn * NEAR, xn, tok_rows, width), bf16),
             pltpu.VMEM((2, tok_rows, model_width), bf16),
-            dma((2,)),
-            dma((8,)),
+            dma((2, xn)),
+            dma((6 + 2 * xn,)),
             dma((len(KINDS),)),
             dma((gn, 2)),
-            dma((2,)),
+            dma((gn, 2)),
             dma((1,)),
             dma((1,)),
             dma((2,)),
+            dma((2, 3)),
             dma((2,)),
             dma((1,)),
             dma((gn,)),
             dma((1,)),
         ],
         compiler_params=pltpu.CompilerParams(
-            collective_id=0, has_side_effects=True, vmem_limit_bytes=40 * 1024 * 1024
+            collective_id=0, has_side_effects=True, vmem_limit_bytes=44 * 1024 * 1024
         ),
     )(
         *(
@@ -747,7 +884,7 @@
     dp_count, expert_count = lax.axis_size("dp"), lax.axis_size("expert")
     whole_heads = groups % expert_count == 0 and pairs_dev == groups // expert_count * E
     small = args[4].shape[2] <= 128
-    if whole_heads and small and expert_count > 1 and dp_count > 1 and args[0].shape[2] % (dp_count * 256) == 0:
+    if whole_heads and small and expert_count > 1 and dp_count % NEAR == 0 and dp_count > NEAR and args[0].shape[2] % (dp_count * 256) == 0:
         return fused(*args)
     return local(*args)
 

time: 45 us -> 39.6 us (0.88)
  the two profiles are of different devices: /device:TPU:1 before, /device:TPU:0 now
where the time goes in v4:
time: 39.6 us; the launch traced here: 39.5 us
  Pallas kernels  38.8 us (98%)
  between operations  0.64 us (2%)
    pallas_call x1, Pallas kernels, fused(): pl.pallas_call(functools.partial(fused_kernel, (dn, gn, jn, own_heads, qu...  35.5 us
    pallas_call x1, Pallas kernels, fused(): pl.pallas_call(finish_kernel, name='finish', out_shape=(jax.ShapeDtypeStr...  3.36 us

profile of v4, /device:TPU:0, one launch (start us, length us, event | category | flops | bytes accessed | tf_op | source)
XLA Modules:
  0.0 39.5 jit_solution(2343386169930262390)
XLA Ops:
  0.6 35.5 %fused.1 = (bf16[8,4096]{1,0:T(8,128)(2,1)S(1)}, bf16[2,4,32,128]{3,2,1,0:T(8,128)(2,1)S(1)}, bf16[2,4,32,128]{3,2,1,0:T(8,128)(2,1)S(1)}, bf16[16,1024,128]{2,1,0:T(8,128)(2,1)S(1)}, bf16[16,1024,128]{2,1,0:T(8,128)(2,1)S(1)}) custom-call(bf16[8,4096]{1,0:T(8,128)(2,1)} %bitcast.13, bf16[8,4096]{1,0:T(8,128)(2,1)} %bitcast.14, ...), custom_call_target="tpu_custom_call" | custom-call | tf_op jit(solution)/shard_map/fused/pallas_call | solution.py:780
  36.1 3.4 %finish.1 = (bf16[8,4096]{1,0:T(8,128)(2,1)}, bf16[32,8,128]{2,1,0:T(8,128)(2,1)}, bf16[32,8,128]{2,1,0:T(8,128)(2,1)}, bf16[16,1024,128]{2,1,0:T(8,128)(2,1)}, bf16[16,1024,128]{2,1,0:T(8,128)(2,1)}) custom-call(bf16[8,4096]{1,0:T(8,128)(2,1)S(1)} %get-tuple-element.15.tok_in, bf16[8,32,128]{2,1,0:T(8,128)(2,1)S(1)} %bitcast.11, ...), custom_call_target="tpu_custom_call" | custom-call | tf_op jit(solution)/shard_map/finish/pallas_call | solution.py:855

commit v5 on v4

--- a/solution.py
+++ b/solution.py
@@ -255,6 +255,7 @@
     routes,
     route_columns,
     weight,
+    turned_weight,
     heads_in,
     part,
     part_in,
@@ -585,9 +586,16 @@
     arrived(routes.at[pl.ds(0, dn - 1)], sem_routes.at[0])
     for b in range(dn):
         turn_routes(b)
+    for copy in weights_on_way[xn:]:
+        copy.wait()
+    for p in range(own_heads * E):
+        for q in range(xn):
+            turned_weight[p // 2, q, (p % 2) * head_dim : (p % 2 + 1) * head_dim, :] = weight[
+                0, p, q
+            ].T
+    relay(0, slice(1, 2))
     from_side(1, slice(0, gn))
     flatten(1)
-    relay(0, slice(1, 2))
     for copy in weights_on_way[:xn]:
         copy.wait()
     project(1)
@@ -599,19 +607,17 @@
     spread(0)
     near_factor(0)
     mask(0, range(0, 1))
-    for copy in weights_on_way[xn:]:
-        copy.wait()
     couples = own_heads * E // 2
     step = min(width, 256)
     for q in range(xn):
         for n in range(0, width, step):
             added = jnp.zeros((cn * seq_len, step), f32)
             for m in range(couples):
-                both = jnp.concatenate(
-                    [weight[0, 2 * m, q, n : n + step, :], weight[0, 2 * m + 1, q, n : n + step, :]],
-                    axis=1,
+                added = added + jnp.dot(
+                    masked[0, m, own_span(x), :],
+                    turned_weight[m, q, :, n : n + step],
+                    preferred_element_type=f32,
                 )
-                added = added + across_rows(masked[0, m, own_span(x), :], both)
             for b in range(cn):
                 for r in range(sources):
                     first = b * seq_len + r * tok_rows
@@ -683,8 +689,8 @@
     on_line(functools.partial(join_halves, slice(2, gn - 1)))
     gather_columns(0)
     hand_over(1)
+    gradients(0, vg_out)
     on_line(functools.partial(join_halves, slice(gn - 1, gn)))
-    gradients(0, vg_out)
     near_factor(1)
     mask(1, range(0, 1))
     gather_columns(1)
@@ -802,6 +808,7 @@
             pltpu.VMEM((dn, 2 * own_heads, 1, seq_len), jnp.int32),
             pltpu.VMEM((dn, -(-seq_len // 128) * 128, 2 * own_heads), jnp.int32),
             pltpu.VMEM((2, pairs_dev, xn, width, head_dim), bf16),
+            pltpu.VMEM((pairs_dev // 2, xn, 2 * head_dim, width), bf16),
             pltpu.VMEM((2, jn, own_heads, query_rows, head_dim), bf16),
             pltpu.VMEM((NEAR, 2, own_heads, seq_len, head_dim), bf16),
             pltpu.VMEM((NEAR, 2, own_heads, seq_len, head_dim), bf16),
@@ -832,7 +839,7 @@
             dma((1,)),
         ],
         compiler_params=pltpu.CompilerParams(
-            collective_id=0, has_side_effects=True, vmem_limit_bytes=44 * 1024 * 1024
+            collective_id=0, has_side_effects=True, vmem_limit_bytes=48 * 1024 * 1024
         ),
     )(
         *(

time: 39.6 us -> 37.2 us (0.939)
  Pallas kernels: 38.8 us -> 36.1 us
    pallas_call x1, Pallas kernels: 35.5 us -> 32.7 us  [fused(): pl.pallas_call(functools.partial(fused_kernel, (dn, gn, jn, own_heads, qu...]
where the time goes in v5:
time: 37.2 us; the launch traced here: 36.7 us
  Pallas kernels  36.1 us (97%)
  between operations  0.64 us (2%)
    pallas_call x1, Pallas kernels, fused(): pl.pallas_call(functools.partial(fused_kernel, (dn, gn, jn, own_heads, qu...  32.7 us
    pallas_call x1, Pallas kernels, fused(): pl.pallas_call(finish_kernel, name='finish', out_shape=(jax.ShapeDtypeStr...  3.36 us

profile of v5, /device:TPU:0, one launch (start us, length us, event | category | flops | bytes accessed | tf_op | source)
XLA Modules:
  0.0 36.7 jit_solution(9762196767357720007)
XLA Ops:
  0.6 32.7 %fused.1 = (bf16[8,4096]{1,0:T(8,128)(2,1)S(1)}, bf16[2,4,32,128]{3,2,1,0:T(8,128)(2,1)S(1)}, bf16[2,4,32,128]{3,2,1,0:T(8,128)(2,1)S(1)}, bf16[16,1024,128]{2,1,0:T(8,128)(2,1)S(1)}, bf16[16,1024,128]{2,1,0:T(8,128)(2,1)S(1)}) custom-call(bf16[8,4096]{1,0:T(8,128)(2,1)} %bitcast.13, bf16[8,4096]{1,0:T(8,128)(2,1)} %bitcast.14, ...), custom_call_target="tpu_custom_call" | custom-call | tf_op jit(solution)/shard_map/fused/pallas_call | solution.py:786
  33.4 3.4 %finish.1 = (bf16[8,4096]{1,0:T(8,128)(2,1)}, bf16[32,8,128]{2,1,0:T(8,128)(2,1)}, bf16[32,8,128]{2,1,0:T(8,128)(2,1)}, bf16[16,1024,128]{2,1,0:T(8,128)(2,1)}, bf16[16,1024,128]{2,1,0:T(8,128)(2,1)}) custom-call(bf16[8,4096]{1,0:T(8,128)(2,1)S(1)} %get-tuple-element.15.tok_in, bf16[8,32,128]{2,1,0:T(8,128)(2,1)S(1)} %bitcast.11, ...), custom_call_target="tpu_custom_call" | custom-call | tf_op jit(solution)/shard_map/finish/pallas_call | solution.py:862

commit v6 on v5

--- a/solution.py
+++ b/solution.py
@@ -624,18 +624,24 @@
                     term[r % jn, r // jn, b, q, :, n : n + step] = added[
                         first : first + tok_rows
                     ].astype(bf16)
-    for target in range(gn):
-        for jj in range(1, jn):
-            send(
-                "half",
-                term.at[lax.rem(j + jj, jn), target],
-                term_side.at[jj, target],
-                sem_half.at[target],
-                at(0, 0, jj),
-            )
+    def turns(k):
+        return [0] + sorted(range(1, gn), key=lambda t: -abs(t - k))
+
+    def send_halves(k):
+        for target in turns(k):
+            for jj in range(1, jn):
+                send(
+                    "half",
+                    term.at[lax.rem(j + jj, jn), target],
+                    term_side.at[jj, target],
+                    sem_half.at[target],
+                    at(0, 0, jj),
+                )
+
+    on_line(send_halves)
 
     def join_halves(which, k):
-        for target in range(gn)[which]:
+        for target in turns(k)[which]:
             arrived(term_side.at[pl.ds(0, jn - 1), target], sem_half.at[target])
             whole = term[j, target].astype(f32)
             for jj in range(1, jn):
@@ -682,18 +688,18 @@
             out[2 * m + 1] = whole[:, head_dim:].astype(bf16)
 
 
+    gather_columns(1)
     hand_over(0)
     on_line(functools.partial(join_halves, slice(1, 2)))
     far_factor(0)
     mask(0, range(1, xn))
+    near_factor(1)
+    mask(1, range(0, 1))
     on_line(functools.partial(join_halves, slice(2, gn - 1)))
     gather_columns(0)
     hand_over(1)
     gradients(0, vg_out)
     on_line(functools.partial(join_halves, slice(gn - 1, gn)))
-    near_factor(1)
-    mask(1, range(0, 1))
-    gather_columns(1)
     far_factor(1)
     mask(1, range(1, xn))
     gradients(1, og_out)

time: 37.2 us -> 36.9 us (level)
  no operation moved by 1% of the time
where the time goes in v6:
time: 36.9 us; the launch traced here: 36.7 us
  Pallas kernels  36.1 us (98%)
  between operations  0.64 us (2%)
    pallas_call x1, Pallas kernels, fused(): pl.pallas_call(functools.partial(fused_kernel, (dn, gn, jn, own_heads, qu...  32.7 us
    pallas_call x1, Pallas kernels, fused(): pl.pallas_call(finish_kernel, name='finish', out_shape=(jax.ShapeDtypeStr...  3.36 us

profile of v6, /device:TPU:0, one launch (start us, length us, event | category | flops | bytes accessed | tf_op | source)
XLA Modules:
  0.0 36.7 jit_solution(17048682370299874744)
XLA Ops:
  0.6 32.7 %fused.1 = (bf16[8,4096]{1,0:T(8,128)(2,1)S(1)}, bf16[2,4,32,128]{3,2,1,0:T(8,128)(2,1)S(1)}, bf16[2,4,32,128]{3,2,1,0:T(8,128)(2,1)S(1)}, bf16[16,1024,128]{2,1,0:T(8,128)(2,1)S(1)}, bf16[16,1024,128]{2,1,0:T(8,128)(2,1)S(1)}) custom-call(bf16[8,4096]{1,0:T(8,128)(2,1)} %bitcast.13, bf16[8,4096]{1,0:T(8,128)(2,1)} %bitcast.14, ...), custom_call_target="tpu_custom_call" | custom-call | tf_op jit(solution)/shard_map/fused/pallas_call | solution.py:792
  33.3 3.4 %finish.1 = (bf16[8,4096]{1,0:T(8,128)(2,1)}, bf16[32,8,128]{2,1,0:T(8,128)(2,1)}, bf16[32,8,128]{2,1,0:T(8,128)(2,1)}, bf16[16,1024,128]{2,1,0:T(8,128)(2,1)}, bf16[16,1024,128]{2,1,0:T(8,128)(2,1)}) custom-call(bf16[8,4096]{1,0:T(8,128)(2,1)S(1)} %get-tuple-element.15.tok_in, bf16[8,32,128]{2,1,0:T(8,128)(2,1)S(1)} %bitcast.11, ...), custom_call_target="tpu_custom_call" | custom-call | tf_op jit(solution)/shard_map/finish/pallas_call | solution.py:868

commit v7 on v6

--- a/solution.py
+++ b/solution.py
@@ -681,8 +681,8 @@
     for jj in range(1, jn):
         send("back", back.at[lax.rem(j + jj, jn)], back_in.at[j], sem_back.at[0], at(0, 0, jj))
 
-    def gradients(i, out):
-        for m in range(couples):
+    def gradients(i, out, some):
+        for m in some:
             whole = jnp.dot(flat_t[i], masked[i, m], preferred_element_type=f32)
             out[2 * m] = whole[:, :head_dim].astype(bf16)
             out[2 * m + 1] = whole[:, head_dim:].astype(bf16)
@@ -698,11 +698,12 @@
     on_line(functools.partial(join_halves, slice(2, gn - 1)))
     gather_columns(0)
     hand_over(1)
-    gradients(0, vg_out)
+    gradients(0, vg_out, range(0, couples * 3 // 4))
     on_line(functools.partial(join_halves, slice(gn - 1, gn)))
+    gradients(0, vg_out, range(couples * 3 // 4, couples))
     far_factor(1)
     mask(1, range(1, xn))
-    gradients(1, og_out)
+    gradients(1, og_out, range(couples))
 
     back_in[j] = back[j]
     arrived(back_in.at[pl.ds(0, jn - 1)], sem_back.at[0])
@@ -741,7 +742,7 @@
 def finish_kernel(
     tok_in, qg_in, kg_in, vg_in, og_in, tok_out, qg_out, kg_out, vg_out, og_out, turned, sems
 ):
-    pieces = E
+    pieces = vg_in.shape[0]
     size = vg_in.shape[0] // pieces
     whole = [
         pltpu.make_async_copy(source, out, sems.at[i])

time: 36.9 us -> 36.7 us (level)
  no operation moved by 1% of the time
where the time goes in v7:
time: 36.7 us; the launch traced here: 36.5 us
  Pallas kernels  35.9 us (98%)
  between operations  0.64 us (2%)
    pallas_call x1, Pallas kernels, fused(): pl.pallas_call(functools.partial(fused_kernel, (dn, gn, jn, own_heads, qu...  32.6 us
    pallas_call x1, Pallas kernels, fused(): pl.pallas_call(finish_kernel, name='finish', out_shape=(jax.ShapeDtypeStr...  3.34 us

profile of v7, /device:TPU:0, one launch (start us, length us, event | category | flops | bytes accessed | tf_op | source)
XLA Modules:
  0.0 36.5 jit_solution(8656584023207934503)
XLA Ops:
  0.6 32.6 %fused.1 = (bf16[8,4096]{1,0:T(8,128)(2,1)S(1)}, bf16[2,4,32,128]{3,2,1,0:T(8,128)(2,1)S(1)}, bf16[2,4,32,128]{3,2,1,0:T(8,128)(2,1)S(1)}, bf16[16,1024,128]{2,1,0:T(8,128)(2,1)S(1)}, bf16[16,1024,128]{2,1,0:T(8,128)(2,1)S(1)}) custom-call(bf16[8,4096]{1,0:T(8,128)(2,1)} %bitcast.13, bf16[8,4096]{1,0:T(8,128)(2,1)} %bitcast.14, ...), custom_call_target="tpu_custom_call" | custom-call | tf_op jit(solution)/shard_map/fused/pallas_call | solution.py:793
  33.2 3.3 %finish.1 = (bf16[8,4096]{1,0:T(8,128)(2,1)}, bf16[32,8,128]{2,1,0:T(8,128)(2,1)}, bf16[32,8,128]{2,1,0:T(8,128)(2,1)}, bf16[16,1024,128]{2,1,0:T(8,128)(2,1)}, bf16[16,1024,128]{2,1,0:T(8,128)(2,1)}) custom-call(bf16[8,4096]{1,0:T(8,128)(2,1)S(1)} %get-tuple-element.15.tok_in, bf16[8,32,128]{2,1,0:T(8,128)(2,1)S(1)} %bitcast.11, ...), custom_call_target="tpu_custom_call" | custom-call | tf_op jit(solution)/shard_map/finish/pallas_call | solution.py:869
